TPU v7x, 512 devices: a whole 4x8x8 slice. The times are simulated.
512 devices in a mesh: row: 32 (over x, y), col: 16 (over z, core).
Axes of the slice: x: 4, y: 8, z: 8, core: 2. Of those that a mesh axis runs over, the one named last changes fastest.
Arguments:
- rhs: bfloat16 [5, 32, 32, 256], P(None, 'row'), may hold values from -6 to 6
- factor: bfloat16 [10, 32, 32, 256, 256], P(None, 'col', 'row'), may hold values from -0.0625 to 0.0625
- pattern: int32 [10, 32, 32], P(None, 'col', 'row'), may hold values 0 or 1
- diag_inverse: bfloat16 [5, 32, 256, 256], P(None, 'row'), as said below
Outputs:
- forward: bfloat16 [5, 32, 32, 256], P(None, 'row')
- solution: bfloat16 [5, 32, 32, 256], P(None, 'row')
Inputs may be any that keep to these rules, and one draw needn't show every extreme that they name: Each block of diag_inverse is lower triangular with a positive diagonal.
All inputs are finite; a program needn't handle non-finite values. No bound on the sum of `pattern` on one device may be relied on, other than what follows from the above.
Results may differ from a plain program's by a relative error of at most 0.028.
Values may be sent and summed in bfloat16 or wider, within the bound.
A program may use at most 64 MiB of HBM per device.

v0:
```python
import jax
import jax.numpy as jnp
from jax import lax
from jax.sharding import PartitionSpec as P


def sent_to_all(array, axis):
    copies = jnp.broadcast_to(array, (lax.axis_size(axis), *array.shape))
    return lax.all_to_all(copies, axis, split_axis=0, concat_axis=0, tiled=True)


def over_copies(array, axis):
    everything = sent_to_all(array, axis)
    return jnp.sum(everything.astype(jnp.float32), axis=0)


def broadcast(array, axis, root):
    return lax.dynamic_index_in_dim(lax.all_gather(array, axis), root, 0, keepdims=False)


def laid_out(blocks, dim):
    blocks = jnp.moveaxis(blocks, 0, dim)
    shape = blocks.shape
    return blocks.reshape(*shape[:dim], shape[dim] * shape[dim + 1], *shape[dim + 2 :])


def gather_directly(array, axis, dim):
    return laid_out(sent_to_all(array, axis), dim)


def pair_index(later, earlier):
    return later * (later - 1) // 2 + earlier


def lower_term(blocks, mask_blocks, solved):
    prod = jnp.einsum("tsij,srj->tsri", blocks, solved, preferred_element_type=jnp.float32)
    return jnp.sum(prod * mask_blocks.astype(jnp.float32)[:, :, None, None], axis=1)


def upper_term(blocks, mask_blocks, solved_rows):
    prod = jnp.einsum("tri,tsij->tsrj", solved_rows, blocks, preferred_element_type=jnp.float32)
    return jnp.sum(prod * mask_blocks.astype(jnp.float32)[:, :, None, None], axis=0)


def solve_lower(zeta, inverse):
    return jnp.einsum("mrj,mij->mri", zeta, inverse, preferred_element_type=jnp.float32).astype(
        jnp.bfloat16
    )


def solve_upper(zeta, inverse):
    return jnp.einsum("mri,mij->mrj", zeta, inverse, preferred_element_type=jnp.float32).astype(
        jnp.bfloat16
    )


def on_device(rhs, factor, pattern, diag_inverse):
    levels = rhs.shape[0]
    own = rhs.shape[1]
    block_rows = factor.shape[1]
    ratio = lax.axis_size("row") // lax.axis_size("col")
    row_id = lax.axis_index("row")
    col_id = lax.axis_index("col")

    def fterm(later, earlier, solved):
        index = pair_index(later, earlier)
        return lower_term(factor[index], pattern[index], solved)

    forward_list = [solve_lower(rhs[0], diag_inverse[0])]
    for level in range(1, levels):
        partial_value = fterm(level, 0, forward_list[0])
        for earlier in range(1, level):
            partial_value = partial_value + fterm(level, earlier, forward_list[earlier])
        finish_total = over_copies(partial_value.astype(jnp.bfloat16), "row").astype(jnp.float32)
        offset = row_id % ratio * own
        mine = lax.dynamic_slice_in_dim(finish_total, offset, own, 0)
        arrived = broadcast(mine.astype(jnp.bfloat16), "col", row_id // ratio).astype(mine.dtype)
        finish_zeta = (rhs[level].astype(jnp.float32) - arrived).astype(jnp.bfloat16)
        forward_list.append(solve_lower(finish_zeta, diag_inverse[level]))

    def spread(solved):
        whole = gather_directly(solved, "row", 0)
        return lax.dynamic_slice_in_dim(whole, col_id * block_rows, block_rows, 0)

    def bterm(later, earlier, spread_rows):
        index = pair_index(later, earlier)
        return upper_term(factor[index], pattern[index], spread_rows)

    back_list = [None] * levels
    spread_list = [None] * levels
    back_list[levels - 1] = solve_upper(forward_list[levels - 1], diag_inverse[levels - 1])
    spread_list[levels - 1] = spread(back_list[levels - 1])
    for level in range(levels - 2, -1, -1):
        partial_value = bterm(levels - 1, level, spread_list[levels - 1])
        for later in range(levels - 2, level, -1):
            partial_value = partial_value + bterm(later, level, spread_list[later])
        total = over_copies(partial_value.astype(jnp.bfloat16), "col").astype(jnp.float32)
        zeta = (forward_list[level].astype(jnp.float32) - total).astype(jnp.bfloat16)
        back_list[level] = solve_upper(zeta, diag_inverse[level])
        if level > 0:
            spread_list[level] = spread(back_list[level])
    return (jnp.stack(forward_list), jnp.stack(back_list))


def solution(mesh):
    return jax.shard_map(
        on_device,
        mesh=mesh,
        in_specs=(
            P(None, "row", None, None),
            P(None, "col", "row", None, None),
            P(None, "col", "row"),
            P(None, "row", None, None),
        ),
        out_specs=(P(None, "row", None, None), P(None, "row", None, None)),
        check_vma=False,
    )
```

profile of v0, /device:TPU:1, one launch (start us, length us, event | category | flops | bytes accessed | tf_op | source)
XLA Modules:
  0.0 391.8 jit_solution(9011117865714066667)
XLA Ops:
  0.7 1.7 convert_reduce_fusion.11
  2.5 1.9 constant_dynamic-update-slice_fusion.4
  4.3 1.1 fusion.40
  5.5 1.2 broadcast_in_dim.24
  6.6 10.6 %all-to-all-start = ((bf16[32,2,32,256]{3,2,1,0:T(8,128)(2,1)}), bf16[32,2,32,256]{3,2,1,0:T(8,128)(2,1)}, u32[]{:S(2)}, u32[]{:S(2)}) async-start(bf16[32,2,32,256]{3,2,1,0:T(8,128)(2,1)} %broadcast_in_dim.24), calls=%async_computation | async-start | bytes 2097152 | tf_op jit(solution)/shard_map/all_to_all | solution.py:9
  17.3 24.8 %all-to-all-done = bf16[32,2,32,256]{3,2,1,0:T(8,128)(2,1)} async-done(((bf16[32,2,32,256]{3,2,1,0:T(8,128)(2,1)}), bf16[32,2,32,256]{3,2,1,0:T(8,128)(2,1)}, u32[]{:S(2)}, u32[]{:S(2)}) %all-to-all-start) | async-done | bytes 1048608 | tf_op jit(solution)/shard_map/all_to_all | solution.py:9
  42.1 1.4 convert_reduce_fusion.3
  43.5 28.4 %all-gather = bf16[16,32,256]{2,1,0:T(8,128)(2,1)S(1)} all-gather(bf16[1,32,256]{2,1,0:T(8,128)(2,1)S(1)} %dynamic-slice_convert_fusion.3), channel_id=2, replica_groups=mesh['row'=32,'col'=16] {'col'}, dimensions={0}, use_global_device_ids=true | all-gather | bytes 278528 | tf_op jit(solution)/shard_map/all_gather | solution.py:18
  71.9 0.8 constant_dynamic-update-slice_fusion.3
  73.1 1.2 broadcast_in_dim.25
  74.3 4.9 %all-to-all-start.1 = ((bf16[32,2,32,256]{3,2,1,0:T(8,128)(2,1)}), bf16[32,2,32,256]{3,2,1,0:T(8,128)(2,1)}, u32[]{:S(2)}, u32[]{:S(2)}) async-start(bf16[32,2,32,256]{3,2,1,0:T(8,128)(2,1)} %broadcast_in_dim.25), calls=%async_computation.1 | async-start | bytes 2097152 | tf_op jit(solution)/shard_map/all_to_all | solution.py:9
  79.4 25.1 %all-to-all-done.1 = bf16[32,2,32,256]{3,2,1,0:T(8,128)(2,1)} async-done(((bf16[32,2,32,256]{3,2,1,0:T(8,128)(2,1)}), bf16[32,2,32,256]{3,2,1,0:T(8,128)(2,1)}, u32[]{:S(2)}, u32[]{:S(2)}) %all-to-all-start.1) | async-done | bytes 1048608 | tf_op jit(solution)/shard_map/all_to_all | solution.py:9
  104.4 1.4 convert_reduce_fusion.2
  105.8 19.0 %all-gather.1 = bf16[16,32,256]{2,1,0:T(8,128)(2,1)S(1)} all-gather(bf16[1,32,256]{2,1,0:T(8,128)(2,1)S(1)} %dynamic-slice_convert_fusion.2), channel_id=3, replica_groups=mesh['row'=32,'col'=16] {'col'}, dimensions={0}, use_global_device_ids=true | all-gather | bytes 278528 | tf_op jit(solution)/shard_map/all_gather | solution.py:18
  126.1 1.2 broadcast_in_dim.26
  127.2 4.9 %all-to-all-start.2 = ((bf16[32,2,32,256]{3,2,1,0:T(8,128)(2,1)}), bf16[32,2,32,256]{3,2,1,0:T(8,128)(2,1)}, u32[]{:S(2)}, u32[]{:S(2)}) async-start(bf16[32,2,32,256]{3,2,1,0:T(8,128)(2,1)} %broadcast_in_dim.26), calls=%async_computation.2 | async-start | bytes 2097152 | tf_op jit(solution)/shard_map/all_to_all | solution.py:9
  132.5 24.9 %all-to-all-done.2 = bf16[32,2,32,256]{3,2,1,0:T(8,128)(2,1)} async-done(((bf16[32,2,32,256]{3,2,1,0:T(8,128)(2,1)}), bf16[32,2,32,256]{3,2,1,0:T(8,128)(2,1)}, u32[]{:S(2)}, u32[]{:S(2)}) %all-to-all-start.2) | async-done | bytes 1048608 | tf_op jit(solution)/shard_map/all_to_all | solution.py:9
  157.4 1.4 convert_reduce_fusion.1
  158.8 21.0 %all-gather.2 = bf16[16,32,256]{2,1,0:T(8,128)(2,1)S(1)} all-gather(bf16[1,32,256]{2,1,0:T(8,128)(2,1)S(1)} %dynamic-slice_convert_fusion.1), channel_id=4, replica_groups=mesh['row'=32,'col'=16] {'col'}, dimensions={0}, use_global_device_ids=true | all-gather | bytes 278528 | tf_op jit(solution)/shard_map/all_gather | solution.py:18
  181.3 0.9 fusion.43
  182.3 29.9 %all_to_all.60 = bf16[32,2,32,256]{3,2,1,0:T(8,128)(2,1)S(1)} all-to-all(bf16[32,2,32,256]{3,2,1,0:T(8,128)(2,1)S(1)} %broadcast_in_dim.27), channel_id=1, replica_groups=mesh['row'=32,'col'=16] {'row'}, dimensions={0} | all-to-all | bytes 2097152 | tf_op jit(solution)/shard_map/all_to_all | solution.py:9
  212.3 19.0 %all-gather.3 = bf16[16,32,256]{2,1,0:T(8,128)(2,1)S(1)} all-gather(bf16[1,32,256]{2,1,0:T(8,128)(2,1)S(1)} %dynamic-slice_convert_fusion), channel_id=5, replica_groups=mesh['row'=32,'col'=16] {'col'}, dimensions={0}, use_global_device_ids=true | all-gather | bytes 278528 | tf_op jit(solution)/shard_map/all_gather | solution.py:18
  232.3 0.9 broadcast_in_dim.28
  233.2 4.9 %all-to-all-start.4 = ((bf16[32,1,32,256]{3,2,1,0:T(8,128)(2,1)}), bf16[32,1,32,256]{3,2,1,0:T(8,128)(2,1)}, u32[]{:S(2)}, u32[]{:S(2)}) async-start(bf16[32,1,32,256]{3,2,1,0:T(8,128)(2,1)} %broadcast_in_dim.28), calls=%async_computation.4 | async-start | bytes 1048576 | tf_op jit(solution)/shard_map/all_to_all | solution.py:9
  238.1 14.7 %all-to-all-done.4 = bf16[32,1,32,256]{3,2,1,0:T(8,128)(2,1)} async-done(((bf16[32,1,32,256]{3,2,1,0:T(8,128)(2,1)}), bf16[32,1,32,256]{3,2,1,0:T(8,128)(2,1)}, u32[]{:S(2)}, u32[]{:S(2)}) %all-to-all-start.4) | async-done | bytes 524320 | tf_op jit(solution)/shard_map/all_to_all | solution.py:9
  252.8 0.9 fusion.28
  253.7 18.5 %all_to_all.61 = bf16[16,1,32,256]{3,2,1,0:T(8,128)(2,1)S(1)} all-to-all(bf16[16,1,32,256]{3,2,1,0:T(8,128)(2,1)S(1)} %broadcast_in_dim.29), channel_id=1, replica_groups=mesh['row'=32,'col'=16] {'col'}, dimensions={0} | all-to-all | bytes 524288 | tf_op jit(solution)/shard_map/all_to_all | solution.py:9
  272.5 0.9 broadcast_in_dim.30
  273.4 5.7 %all-to-all-start.6 = ((bf16[32,1,32,256]{3,2,1,0:T(8,128)(2,1)}), bf16[32,1,32,256]{3,2,1,0:T(8,128)(2,1)}, u32[]{:S(2)}, u32[]{:S(2)}) async-start(bf16[32,1,32,256]{3,2,1,0:T(8,128)(2,1)} %broadcast_in_dim.30), calls=%async_computation.6 | async-start | bytes 1048576 | tf_op jit(solution)/shard_map/all_to_all | solution.py:9
  279.1 0.9 fusion.30
  280.0 15.5 %all-to-all-done.6 = bf16[32,1,32,256]{3,2,1,0:T(8,128)(2,1)} async-done(((bf16[32,1,32,256]{3,2,1,0:T(8,128)(2,1)}), bf16[32,1,32,256]{3,2,1,0:T(8,128)(2,1)}, u32[]{:S(2)}, u32[]{:S(2)}) %all-to-all-start.6) | async-done | bytes 524320 | tf_op jit(solution)/shard_map/all_to_all | solution.py:9
  295.5 0.9 fusion.31
  296.4 15.5 %all_to_all.62 = bf16[16,1,32,256]{3,2,1,0:T(8,128)(2,1)S(1)} all-to-all(bf16[16,1,32,256]{3,2,1,0:T(8,128)(2,1)S(1)} %broadcast_in_dim.31), channel_id=1, replica_groups=mesh['row'=32,'col'=16] {'col'}, dimensions={0} | all-to-all | bytes 524288 | tf_op jit(solution)/shard_map/all_to_all | solution.py:9
  312.1 0.9 broadcast_in_dim.64
  313.0 5.7 %all-to-all-start.8 = ((bf16[32,1,32,256]{3,2,1,0:T(8,128)(2,1)}), bf16[32,1,32,256]{3,2,1,0:T(8,128)(2,1)}, u32[]{:S(2)}, u32[]{:S(2)}) async-start(bf16[32,1,32,256]{3,2,1,0:T(8,128)(2,1)} %broadcast_in_dim.64), calls=%async_computation.8 | async-start | bytes 1048576 | tf_op jit(solution)/shard_map/all_to_all | solution.py:9
  318.7 0.9 fusion.33
  319.6 0.9 fusion.34
  320.6 14.6 %all-to-all-done.8 = bf16[32,1,32,256]{3,2,1,0:T(8,128)(2,1)} async-done(((bf16[32,1,32,256]{3,2,1,0:T(8,128)(2,1)}), bf16[32,1,32,256]{3,2,1,0:T(8,128)(2,1)}, u32[]{:S(2)}, u32[]{:S(2)}) %all-to-all-start.8) | async-done | bytes 524320 | tf_op jit(solution)/shard_map/all_to_all | solution.py:9
  335.2 0.9 fusion.35
  336.2 15.3 %all_to_all.63 = bf16[16,1,32,256]{3,2,1,0:T(8,128)(2,1)S(1)} all-to-all(bf16[16,1,32,256]{3,2,1,0:T(8,128)(2,1)S(1)} %broadcast_in_dim.65), channel_id=1, replica_groups=mesh['row'=32,'col'=16] {'col'}, dimensions={0} | all-to-all | bytes 524288 | tf_op jit(solution)/shard_map/all_to_all | solution.py:9
  351.6 0.9 broadcast_in_dim.66
  352.5 5.6 %all-to-all-start.10 = ((bf16[32,1,32,256]{3,2,1,0:T(8,128)(2,1)}), bf16[32,1,32,256]{3,2,1,0:T(8,128)(2,1)}, u32[]{:S(2)}, u32[]{:S(2)}) async-start(bf16[32,1,32,256]{3,2,1,0:T(8,128)(2,1)} %broadcast_in_dim.66), calls=%async_computation.10 | async-start | bytes 1048576 | tf_op jit(solution)/shard_map/all_to_all | solution.py:9
  358.2 0.9 fusion.27
  359.1 0.9 fusion.29
  360.0 0.9 fusion.32
  360.9 13.7 %all-to-all-done.10 = bf16[32,1,32,256]{3,2,1,0:T(8,128)(2,1)} async-done(((bf16[32,1,32,256]{3,2,1,0:T(8,128)(2,1)}), bf16[32,1,32,256]{3,2,1,0:T(8,128)(2,1)}, u32[]{:S(2)}, u32[]{:S(2)}) %all-to-all-start.10) | async-done | bytes 524320 | tf_op jit(solution)/shard_map/all_to_all | solution.py:9
  374.7 0.9 fusion.36
  375.6 15.3 %all_to_all.64 = bf16[16,1,32,256]{3,2,1,0:T(8,128)(2,1)S(1)} all-to-all(bf16[16,1,32,256]{3,2,1,0:T(8,128)(2,1)S(1)} %broadcast_in_dim.67), channel_id=1, replica_groups=mesh['row'=32,'col'=16] {'col'}, dimensions={0} | all-to-all | bytes 524288 | tf_op jit(solution)/shard_map/all_to_all | solution.py:9
  (81 shorter events, 6.4 us)
Async XLA Ops:
  0.6 71.3 %copy-start.1 = (bf16[5,1,256,256]{3,2,1,0:T(8,128)(2,1)S(1)}, bf16[5,1,256,256]{3,2,1,0:T(8,128)(2,1)}, u32[]{:S(2)}) copy-start(bf16[5,1,256,256]{3,2,1,0:T(8,128)(2,1)} %param.7) | copy-start | bytes 1966084
  0.6 71.3 %copy-start.2 = (bf16[5,1,32,256]{3,2,1,0:T(8,128)(2,1)S(1)}, bf16[5,1,32,256]{3,2,1,0:T(8,128)(2,1)}, u32[]{:S(2)}) copy-start(bf16[5,1,32,256]{3,2,1,0:T(8,128)(2,1)} %param.4) | copy-start | bytes 245764
  2.4 14.9 %copy-start.3 = (f32[2]{0:T(128)}, f32[2]{0:T(128)S(1)}, u32[]{:S(2)}) copy-start(f32[2]{0:T(128)S(1)} %get-tuple-element.9) | copy-start | bytes 28
  2.4 70.3 %copy-start.8 = (f32[2]{0:T(128)}, f32[2]{0:T(128)S(1)}, u32[]{:S(2)}) copy-start(f32[2]{0:T(128)S(1)} %get-tuple-element.7) | copy-start | bytes 28
  2.4 70.5 %copy-start.5 = (f32[2]{0:T(128)}, f32[2]{0:T(128)S(1)}, u32[]{:S(2)}) copy-start(f32[2]{0:T(128)S(1)} %get-tuple-element.8) | copy-start | bytes 28
  2.4 76.8 %copy-start.10 = (f32[2]{0:T(128)}, f32[2]{0:T(128)S(1)}, u32[]{:S(2)}) copy-start(f32[2]{0:T(128)S(1)} %get-tuple-element.5) | copy-start | bytes 28
  2.4 123.3 %copy-start.14 = (f32[2]{0:T(128)}, f32[2]{0:T(128)S(1)}, u32[]{:S(2)}) copy-start(f32[2]{0:T(128)S(1)} %get-tuple-element.4) | copy-start | bytes 28
  2.4 123.4 %copy-start.18 = (f32[2]{0:T(128)}, f32[2]{0:T(128)S(1)}, u32[]{:S(2)}) copy-start(f32[2]{0:T(128)S(1)} %get-tuple-element.6) | copy-start | bytes 28
  2.4 129.7 %copy-start.12 = (f32[2]{0:T(128)}, f32[2]{0:T(128)S(1)}, u32[]{:S(2)}) copy-start(f32[2]{0:T(128)S(1)} %get-tuple-element.3) | copy-start | bytes 28
  2.4 129.9 %copy-start.16 = (f32[2]{0:T(128)}, f32[2]{0:T(128)S(1)}, u32[]{:S(2)}) copy-start(f32[2]{0:T(128)S(1)} %get-tuple-element.11) | copy-start | bytes 28
  2.4 70.3 %copy-start = (bf16[10,2,1,256,256]{4,3,2,1,0:T(8,128)(2,1)S(1)}, bf16[10,2,1,256,256]{4,3,2,1,0:T(8,128)(2,1)}, u32[]{:S(2)}) copy-start(bf16[10,2,1,256,256]{4,3,2,1,0:T(8,128)(2,1)} %param.5) | copy-start | bytes 7864324
  6.6 35.5 %all-to-all-start = ((bf16[32,2,32,256]{3,2,1,0:T(8,128)(2,1)}), bf16[32,2,32,256]{3,2,1,0:T(8,128)(2,1)}, u32[]{:S(2)}, u32[]{:S(2)}) async-start(bf16[32,2,32,256]{3,2,1,0:T(8,128)(2,1)} %broadcast_in_dim.24), calls=%async_computation | async-start | bytes 2097152 | tf_op jit(solution)/shard_map/all_to_all | solution.py:9
  74.3 30.2 %all-to-all-start.1 = ((bf16[32,2,32,256]{3,2,1,0:T(8,128)(2,1)}), bf16[32,2,32,256]{3,2,1,0:T(8,128)(2,1)}, u32[]{:S(2)}, u32[]{:S(2)}) async-start(bf16[32,2,32,256]{3,2,1,0:T(8,128)(2,1)} %broadcast_in_dim.25), calls=%async_computation.1 | async-start | bytes 2097152 | tf_op jit(solution)/shard_map/all_to_all | solution.py:9
  127.2 30.2 %all-to-all-start.2 = ((bf16[32,2,32,256]{3,2,1,0:T(8,128)(2,1)}), bf16[32,2,32,256]{3,2,1,0:T(8,128)(2,1)}, u32[]{:S(2)}, u32[]{:S(2)}) async-start(bf16[32,2,32,256]{3,2,1,0:T(8,128)(2,1)} %broadcast_in_dim.26), calls=%async_computation.2 | async-start | bytes 2097152 | tf_op jit(solution)/shard_map/all_to_all | solution.py:9
  182.3 70.5 %copy-start.21 = (f32[2]{0:T(128)S(1)}, f32[2]{0:T(128)}, u32[]{:S(2)}) copy-start(f32[2]{0:T(128)} %get-tuple-element.10) | copy-start | bytes 28
  231.4 47.7 %copy-start.17 = (f32[2]{0:T(128)S(1)}, f32[2]{0:T(128)}, u32[]{:S(2)}) copy-start(f32[2]{0:T(128)} %copy-done.16) | copy-start | bytes 28
  232.2 63.3 %copy-start.15 = (f32[2]{0:T(128)S(1)}, f32[2]{0:T(128)}, u32[]{:S(2)}) copy-start(f32[2]{0:T(128)} %copy-done.14) | copy-start | bytes 28
  233.2 19.6 %all-to-all-start.4 = ((bf16[32,1,32,256]{3,2,1,0:T(8,128)(2,1)}), bf16[32,1,32,256]{3,2,1,0:T(8,128)(2,1)}, u32[]{:S(2)}, u32[]{:S(2)}) async-start(bf16[32,1,32,256]{3,2,1,0:T(8,128)(2,1)} %broadcast_in_dim.28), calls=%async_computation.4 | async-start | bytes 1048576 | tf_op jit(solution)/shard_map/all_to_all | solution.py:9
  272.5 46.2 %copy-start.13 = (f32[2]{0:T(128)S(1)}, f32[2]{0:T(128)}, u32[]{:S(2)}) copy-start(f32[2]{0:T(128)} %copy-done.12) | copy-start | bytes 28
  273.4 46.3 %copy-start.11 = (f32[2]{0:T(128)S(1)}, f32[2]{0:T(128)}, u32[]{:S(2)}) copy-start(f32[2]{0:T(128)} %copy-done.10) | copy-start | bytes 28
  273.4 61.8 %copy-start.9 = (f32[2]{0:T(128)S(1)}, f32[2]{0:T(128)}, u32[]{:S(2)}) copy-start(f32[2]{0:T(128)} %copy-done.8) | copy-start | bytes 28
  273.4 22.1 %all-to-all-start.6 = ((bf16[32,1,32,256]{3,2,1,0:T(8,128)(2,1)}), bf16[32,1,32,256]{3,2,1,0:T(8,128)(2,1)}, u32[]{:S(2)}, u32[]{:S(2)}) async-start(bf16[32,1,32,256]{3,2,1,0:T(8,128)(2,1)} %broadcast_in_dim.30), calls=%async_computation.6 | async-start | bytes 1048576 | tf_op jit(solution)/shard_map/all_to_all | solution.py:9
  313.0 45.2 %copy-start.7 = (f32[2]{0:T(128)S(1)}, f32[2]{0:T(128)}, u32[]{:S(2)}) copy-start(f32[2]{0:T(128)} %get-tuple-element.2) | copy-start | bytes 28
  313.0 46.1 %copy-start.19 = (f32[2]{0:T(128)S(1)}, f32[2]{0:T(128)}, u32[]{:S(2)}) copy-start(f32[2]{0:T(128)} %copy-done.18) | copy-start | bytes 28
  313.0 47.0 %copy-start.6 = (f32[2]{0:T(128)S(1)}, f32[2]{0:T(128)}, u32[]{:S(2)}) copy-start(f32[2]{0:T(128)} %copy-done.5) | copy-start | bytes 28
  313.0 22.2 %all-to-all-start.8 = ((bf16[32,1,32,256]{3,2,1,0:T(8,128)(2,1)}), bf16[32,1,32,256]{3,2,1,0:T(8,128)(2,1)}, u32[]{:S(2)}, u32[]{:S(2)}) async-start(bf16[32,1,32,256]{3,2,1,0:T(8,128)(2,1)} %broadcast_in_dim.64), calls=%async_computation.8 | async-start | bytes 1048576 | tf_op jit(solution)/shard_map/all_to_all | solution.py:9
  318.7 56.0 %copy-start.4 = (f32[2]{0:T(128)S(1)}, f32[2]{0:T(128)}, u32[]{:S(2)}) copy-start(f32[2]{0:T(128)} %copy-done.3) | copy-start | bytes 28
  352.5 22.1 %all-to-all-start.10 = ((bf16[32,1,32,256]{3,2,1,0:T(8,128)(2,1)}), bf16[32,1,32,256]{3,2,1,0:T(8,128)(2,1)}, u32[]{:S(2)}, u32[]{:S(2)}) async-start(bf16[32,1,32,256]{3,2,1,0:T(8,128)(2,1)} %broadcast_in_dim.66), calls=%async_computation.10 | async-start | bytes 1048576 | tf_op jit(solution)/shard_map/all_to_all | solution.py:9
  391.1 0.6 copy-start.20
where the time goes:
time: 394 us; the launch traced here: 392 us
  blocking collectives  182 us (46%)
  waiting for transfers between devices  133 us (34%)
  starting transfers between devices  42.5 us (11%)
  matrix products  18.8 us (5%)
  local copies, waits for them, and re-layouts  8.05 us (2%)
  other arithmetic  6.25 us (2%)
    all_to_all x7, waiting for transfers between devices, sent_to_all(): return lax.all_to_all(copies, axis, split_axis=0, concat_axis=0, tiled=True)  133 us
    all_to_all x5, blocking collectives, sent_to_all(): return lax.all_to_all(copies, axis, split_axis=0, concat_axis=0, tiled=True)  94.4 us
    all_gather x4, blocking collectives, broadcast(): lax.all_gather(array, axis)  87.4 us
    all_to_all x7, starting transfers between devices, sent_to_all(): return lax.all_to_all(copies, axis, split_axis=0, concat_axis=0, tiled=True)  42.5 us
    dot_general x10, matrix products, upper_term(): jnp.einsum('tri,tsij->tsrj', solved_rows, blocks, preferred_element_type=...  9.16 us
  transfers between devices with their start and end apart: 7, of which 7 were waited for; matrix products, arithmetic and copies ran while one was open for 2% of the time, Pallas kernels for 0%

commit v1 on v0

v1 whole, which is shorter than its diff:
```python
import functools

import jax
import jax.numpy as jnp
from jax import lax
from jax.experimental import pallas as pl
from jax.experimental.pallas import tpu as pltpu
from jax.sharding import PartitionSpec as P

MESH = pl.DeviceIdType.MESH
BF16 = jnp.bfloat16
F32 = jnp.float32


def pair_index(later, earlier):
    return later * (later - 1) // 2 + earlier


def times_transposed(left, right):
    return lax.dot_general(left, right, (((1,), (1,)), ((), ())), preferred_element_type=F32)


def times(left, right):
    return lax.dot_general(left, right, (((1,), (0,)), ((), ())), preferred_element_type=F32)


def kernel(
    levels, rows, cols,
    rhs, factor, pattern, diag, forward_out, solution_out,
    fsend, arecv, fbuf, usend, rrecv, sbuf, pbuf,
    a_send, a_recv, b_send, b_recv, r_send, r_recv, p_send, p_recv, s_send, s_recv,
):
    row = lax.axis_index("row")
    col = lax.axis_index("col")
    core = col % 2
    chip = col // 2
    home_col = row // 2
    home_chip = home_col // 2
    at_home = chip == home_chip
    own_slot = row % 2
    is_self = at_home & (col == home_col)
    half = fsend.shape[3]
    width = rhs.shape[-1]

    def remote(src, dst, send_sem, recv_sem, device):
        return pltpu.make_async_remote_copy(
            src_ref=src, dst_ref=dst, send_sem=send_sem, recv_sem=recv_sem, device_id=device, device_id_type=MESH
        )

    def send(src, dst, send_sem, recv_sem, device):
        same = (device[0] == row) & (device[1] == col)

        @pl.when(same)
        def _():
            pltpu.make_async_copy(src, dst, recv_sem).start()

        @pl.when(jnp.logical_not(same))
        def _():
            remote(src, dst, send_sem, recv_sem, device).start()

    def await_recv(ref, sem):
        remote(ref, ref, sem, sem, (row, col)).wait_recv()

    def await_send(count, sem):
        ref = arecv.at[0, pl.ds(0, count)]
        remote(ref, ref, sem, sem, (row, col)).wait_send()

    barrier = pltpu.get_barrier_semaphore()

    def greet(device):
        same = (device[0] == row) & (device[1] == col)

        @pl.when(jnp.logical_not(same))
        def _():
            pl.semaphore_signal(barrier, inc=1, device_id=device, device_id_type=MESH)

    for h in range(2):
        greet((row, home_chip * 2 + h))
        for j in range(2):
            greet((2 * col + j, chip * 2 + h))

    @pl.when(at_home)
    def _():
        def along_rows(i, _):
            greet(((row + i) % rows, home_col))
            return 0

        def along_cols(i, _):
            greet((row, (col + i) % cols))
            return 0

        lax.fori_loop(0, rows, along_rows, 0)
        lax.fori_loop(1, cols, along_cols, 0)

    def mask(index, j):
        return pattern[index, j, 0].astype(F32)

    def both(ref):
        return ref[...].reshape(2 * half, width)

    def fterm(later, earlier, j):
        index = pair_index(later, earlier)
        return times_transposed(both(fbuf.at[earlier]), factor[2 * index + j]) * mask(index, j)

    def bterm(later, earlier, j):
        index = pair_index(later, earlier)
        return times(both(pbuf.at[later, j]), factor[2 * index + j]) * mask(index, j)

    def solve_and_spread(level, zeta):
        sbuf[level, core] = times(zeta, diag[level]).astype(BF16)
        if level > 0:

            def along_rows(i, _):
                to = (row + i) % rows
                send(
                    sbuf.at[level, core], pbuf.at[level, own_slot, core],
                    p_send.at[level - 1], p_recv.at[level - 1], (to, home_col),
                )
                return 0

            lax.fori_loop(0, rows, along_rows, 0)

        def along_cols(i, _):
            to = (col + i) % cols
            remote(sbuf.at[level, core], sbuf.at[level, core], s_send.at[level], s_recv.at[level], (row, to)).start()
            return 0

        lax.fori_loop(1, cols, along_cols, 0)

    def await_halves(buf, sem):
        @pl.when(at_home)
        def _():
            await_recv(buf.at[0], sem)

        @pl.when(jnp.logical_not(at_home))
        def _():
            await_recv(buf, sem)

    first = times_transposed(rhs[0], diag[0]).astype(BF16)
    fbuf[0] = first.reshape(2, half, width)
    lower = [fterm(1, 0, j) for j in range(2)]

    for level in range(1, levels):
        at = level - 1
        for j in range(2):
            fsend[at, j] = lower[j].astype(BF16).reshape(2, half, width)
        if level == 1:

            @pl.when(jnp.logical_not(at_home))
            def _():
                pl.semaphore_wait(barrier, 6)

            @pl.when(at_home & jnp.logical_not(is_self))
            def _():
                pl.semaphore_wait(barrier, 5 + rows + cols - 1)

            @pl.when(is_self)
            def _():
                pl.semaphore_wait(barrier, 5 + rows + cols - 1 - 2)

        for j in range(2):
            for h in range(2):
                send(fsend.at[at, j, h], arecv.at[at, row], a_send.at[at], a_recv.at[at], (2 * col + j, chip * 2 + h))

        if level + 1 < levels:
            early = [sum(fterm(level + 1, b, j) for b in range(level)) for j in range(2)]

        @pl.when(at_home)
        def _():
            await_recv(arecv.at[at], a_recv.at[at])
            total = jnp.sum(arecv[at].astype(F32), axis=0)
            zeta = (rhs[level, pl.ds(pl.multiple_of(core * half, half), half)].astype(F32) - total).astype(BF16)
            fbuf[level, core] = times_transposed(zeta, diag[level]).astype(BF16)

            if level == levels - 1:
                solve_and_spread(level, fbuf[level, core])

            def along(i, _):
                to = (col + i) % cols
                remote(fbuf.at[level, core], fbuf.at[level, core], b_send.at[at], b_recv.at[at], (row, to)).start()
                return 0

            lax.fori_loop(1, cols, along, 0)

        if level + 1 < levels:
            await_halves(fbuf.at[level], b_recv.at[at])
            lower = [early[j] + fterm(level + 1, level, j) for j in range(2)]

    early = None
    for level in range(levels - 2, -1, -1):
        await_recv(pbuf.at[level + 1], p_recv.at[level])
        upper = bterm(level + 1, level, 0) + bterm(level + 1, level, 1)
        if early is not None:
            upper = upper + early
        usend[level] = upper.astype(BF16).reshape(2, half, width)
        for h in range(2):
            send(usend.at[level, h], rrecv.at[level, col], r_send.at[level], r_recv.at[level], (row, home_chip * 2 + h))
        if level > 0:
            early = sum(bterm(later, level - 1, j) for later in range(level + 1, levels) for j in range(2))

        @pl.when(at_home)
        def _():
            await_recv(rrecv.at[level], r_recv.at[level])
            total = jnp.sum(rrecv[level].astype(F32), axis=0)
            solve_and_spread(level, (fbuf[level, core].astype(F32) - total).astype(BF16))

    await_halves(fbuf.at[levels - 1], b_recv.at[levels - 2])
    forward_out[...] = fbuf[...].reshape(forward_out.shape)
    for level in range(levels - 1, -1, -1):
        await_halves(sbuf.at[level], s_recv.at[level])
        solution_out[level] = both(sbuf.at[level])

    for at in range(levels - 1):

        @pl.when(is_self)
        def _():
            await_send(3, a_send.at[at])
            await_send(1, r_send.at[at])

        @pl.when(jnp.logical_not(is_self))
        def _():
            await_send(4, a_send.at[at])

            @pl.when(at_home)
            def _():
                await_send(1, r_send.at[at])

            @pl.when(jnp.logical_not(at_home))
            def _():
                await_send(2, r_send.at[at])

        @pl.when(at_home)
        def _():
            await_send(cols - 1, b_send.at[at])

            @pl.when(is_self)
            def _():
                await_send(rows - 1, p_send.at[at])

            @pl.when(jnp.logical_not(is_self))
            def _():
                await_send(rows, p_send.at[at])

    @pl.when(at_home)
    def _():
        for level in range(levels):
            await_send(cols - 1, s_send.at[level])


def on_device(rhs, factor, pattern, diag_inverse):
    levels, _, count, width = rhs.shape
    pairs, block_rows = factor.shape[:2]
    rows, cols = lax.axis_size("row"), lax.axis_size("col")
    half = count // 2
    steps = levels - 1
    vmem = pl.BlockSpec(memory_space=pltpu.VMEM)
    dma = pltpu.SemaphoreType.DMA
    out = jax.ShapeDtypeStruct((levels, count, width), BF16)
    forward, solved = pl.pallas_call(
        functools.partial(kernel, levels, rows, cols),
        out_shape=(out, out),
        in_specs=[vmem, vmem, pl.BlockSpec(memory_space=pltpu.SMEM), vmem],
        out_specs=(vmem, vmem),
        scratch_shapes=[
            pltpu.VMEM((steps, 2, 2, half, width), BF16),
            pltpu.VMEM((steps, rows, half, width), BF16),
            pltpu.VMEM((levels, 2, half, width), BF16),
            pltpu.VMEM((steps, 2, half, width), BF16),
            pltpu.VMEM((steps, cols, half, width), BF16),
            pltpu.VMEM((levels, 2, half, width), BF16),
            pltpu.VMEM((levels, 2, 2, half, width), BF16),
        ]
        + [dma((steps,))] * 8
        + [dma((levels,))] * 2,
        compiler_params=pltpu.CompilerParams(collective_id=0, has_side_effects=True, vmem_limit_bytes=32 << 20),
        name="solves",
    )(
        rhs.reshape(levels, count, width),
        factor.reshape(pairs * block_rows, width, width),
        pattern,
        diag_inverse.reshape(levels, width, width),
    )
    return forward.reshape(rhs.shape), solved.reshape(rhs.shape)


def solution(mesh):
    return jax.shard_map(
        on_device,
        mesh=mesh,
        in_specs=(
            P(None, "row", None, None),
            P(None, "col", "row", None, None),
            P(None, "col", "row"),
            P(None, "row", None, None),
        ),
        out_specs=(P(None, "row", None, None), P(None, "row", None, None)),
        check_vma=False,
    )
```

time: 394 us -> 120 us (0.30)
  the two profiles are of different devices: /device:TPU:1 before, /device:TPU:13 now
where the time goes in v1:
time: 120 us
  Pallas kernels  114 us (95%)
  local copies, waits for them, and re-layouts  5.76 us (5%)
    pallas_call x1, Pallas kernels, on_device(): pl.pallas_call(functools.partial(kernel, levels, rows, cols), out_shape=(...  114 us
    unnamed x9, local copies, waits for them, and re-layouts  5.76 us

profile of v1, /device:TPU:13, one launch (start us, length us, event | category | flops | bytes accessed | tf_op | source)
XLA Modules:
  0.0 120.2 jit_solution(17961784124970102758)
XLA Ops:
  0.6 0.8 copy.6.pattern
  1.4 0.0 copy-start
  1.4 1.7 %copy-done = bf16[10,2,1,256,256]{4,3,2,1,0:T(8,128)(2,1)S(1)} copy-done((bf16[10,2,1,256,256]{4,3,2,1,0:T(8,128)(2,1)S(1)}, bf16[10,2,1,256,256]{4,3,2,1,0:T(8,128)(2,1)}, u32[]{:S(2)}) %copy-start) | copy-done | bytes 2621464
  3.1 0.0 copy-start.1
  3.1 1.1 copy-done.1
  4.2 0.0 copy-start.2
  4.2 0.9 copy-done.2
  5.1 113.8 %solves.1 = (bf16[5,32,256]{2,1,0:T(8,128)(2,1)S(1)}, bf16[5,32,256]{2,1,0:T(8,128)(2,1)S(1)}) custom-call(bf16[5,32,256]{2,1,0:T(8,128)(2,1)S(1)} %bitcast.11, bf16[20,256,256]{2,1,0:T(8,128)(2,1)S(1)} %bitcast.9, s32[10,2,1]{2,1,0:T(2,128)S(1)} %copy.6.pattern, bf16[5,256,256]{2,1,0:T(8,128)(2,1)S(1)} %bitcast.10), custom_call_target="tpu_custom_call" | custom-call | tf_op jit(solution)/shard_map/solves/pallas_call | solution.py:259
  118.9 0.6 copy.11
  119.5 0.6 copy.12
Async XLA Ops:
  1.4 1.7 %copy-start = (bf16[10,2,1,256,256]{4,3,2,1,0:T(8,128)(2,1)S(1)}, bf16[10,2,1,256,256]{4,3,2,1,0:T(8,128)(2,1)}, u32[]{:S(2)}) copy-start(bf16[10,2,1,256,256]{4,3,2,1,0:T(8,128)(2,1)} %param.5) | copy-start | bytes 7864324
  3.1 1.1 copy-start.1
  4.2 0.9 copy-start.2

commit v2 on v1

--- a/solution.py
+++ b/solution.py
@@ -26,9 +26,9 @@
 
 def kernel(
     levels, rows, cols,
-    rhs, factor, pattern, diag, forward_out, solution_out,
-    fsend, arecv, fbuf, usend, rrecv, sbuf, pbuf,
-    a_send, a_recv, b_send, b_recv, r_send, r_recv, p_send, p_recv, s_send, s_recv,
+    rhs_hbm, factor_hbm, pattern, diag_hbm, forward_out, solution_out,
+    rhs, factor, diag, fsend, arecv, fbuf, usend, rrecv, sbuf, pbuf,
+    a_send, a_recv, b_send, b_recv, r_send, r_recv, p_send, p_recv, s_send, s_recv, loaded,
 ):
     row = lax.axis_index("row")
     col = lax.axis_index("col")
@@ -65,6 +65,21 @@
         ref = arecv.at[0, pl.ds(0, count)]
         remote(ref, ref, sem, sem, (row, col)).wait_send()
 
+    loads = [
+        pltpu.make_async_copy(src, dst, loaded.at[n])
+        for n, (src, dst) in enumerate(
+            [
+                (rhs_hbm, rhs),
+                (diag_hbm.at[0], diag.at[0]),
+                (factor_hbm.at[pl.ds(0, 2)], factor.at[pl.ds(0, 2)]),
+                (diag_hbm.at[pl.ds(1, levels - 1)], diag.at[pl.ds(1, levels - 1)]),
+                (factor_hbm.at[pl.ds(2, factor.shape[0] - 2)], factor.at[pl.ds(2, factor.shape[0] - 2)]),
+            ]
+        )
+    ]
+    for load in loads:
+        load.start()
+
     barrier = pltpu.get_barrier_semaphore()
 
     def greet(device):
@@ -74,26 +89,28 @@
         def _():
             pl.semaphore_signal(barrier, inc=1, device_id=device, device_id_type=MESH)
 
+    def around(n, size):
+        return (size // 2 + (1 - 2 * (n % 2)) * ((n + 1) // 2)) % size
+
+    def row_at(n):
+        return (row // 8 + around(n % 4, 4)) % 4 * 8 + (row + around(n // 4, 8)) % 8
+
+    def col_at(n):
+        return (chip + around(n // 2, 8)) % 8 * 2 + (core + 1 - n % 2) % 2
+
+    @pl.when(at_home)
+    def _():
+        def along_rows(n, _):
+            greet((row_at(n), home_col))
+            return 0
+
+        lax.fori_loop(0, rows, along_rows, 0)
+
     for h in range(2):
         greet((row, home_chip * 2 + h))
-        for j in range(2):
-            greet((2 * col + j, chip * 2 + h))
-
-    @pl.when(at_home)
-    def _():
-        def along_rows(i, _):
-            greet(((row + i) % rows, home_col))
-            return 0
-
-        def along_cols(i, _):
-            greet((row, (col + i) % cols))
-            return 0
-
-        lax.fori_loop(0, rows, along_rows, 0)
-        lax.fori_loop(1, cols, along_cols, 0)
 
     def mask(index, j):
-        return pattern[index, j, 0].astype(F32)
+        return pattern[j, 0, index].astype(F32)
 
     def both(ref):
         return ref[...].reshape(2 * half, width)
@@ -108,24 +125,21 @@
 
     def solve_and_spread(level, zeta):
         sbuf[level, core] = times(zeta, diag[level]).astype(BF16)
-        if level > 0:
-
-            def along_rows(i, _):
-                to = (row + i) % rows
-                send(
-                    sbuf.at[level, core], pbuf.at[level, own_slot, core],
-                    p_send.at[level - 1], p_recv.at[level - 1], (to, home_col),
-                )
-                return 0
-
-            lax.fori_loop(0, rows, along_rows, 0)
-
-        def along_cols(i, _):
-            to = (col + i) % cols
-            remote(sbuf.at[level, core], sbuf.at[level, core], s_send.at[level], s_recv.at[level], (row, to)).start()
+        half_solved, at = sbuf.at[level, core], level - 1
+
+        def along_rows(n, _):
+            to = (row_at(n), home_col)
+            remote(half_solved, pbuf.at[level, own_slot, core], p_send.at[at], p_recv.at[at], to).start()
             return 0
 
-        lax.fori_loop(1, cols, along_cols, 0)
+        lax.fori_loop(0, rows - 1, along_rows, 0)
+        send(half_solved, pbuf.at[level, own_slot, core], p_send.at[at], p_recv.at[at], (row, home_col))
+
+        def along_cols(n, _):
+            remote(half_solved, half_solved, s_send.at[level], s_recv.at[level], (row, col_at(n))).start()
+            return 0
+
+        lax.fori_loop(0, cols - 1, along_cols, 0)
 
     def await_halves(buf, sem):
         @pl.when(at_home)
@@ -136,8 +150,11 @@
         def _():
             await_recv(buf, sem)
 
+    loads[0].wait()
+    loads[1].wait()
     first = times_transposed(rhs[0], diag[0]).astype(BF16)
     fbuf[0] = first.reshape(2, half, width)
+    loads[2].wait()
     lower = [fterm(1, 0, j) for j in range(2)]
 
     for level in range(1, levels):
@@ -148,20 +165,23 @@
 
             @pl.when(jnp.logical_not(at_home))
             def _():
-                pl.semaphore_wait(barrier, 6)
+                pl.semaphore_wait(barrier, 4)
 
             @pl.when(at_home & jnp.logical_not(is_self))
             def _():
-                pl.semaphore_wait(barrier, 5 + rows + cols - 1)
+                pl.semaphore_wait(barrier, 4 + cols - 1)
 
             @pl.when(is_self)
             def _():
-                pl.semaphore_wait(barrier, 5 + rows + cols - 1 - 2)
+                pl.semaphore_wait(barrier, 3 + cols - 1)
 
         for j in range(2):
             for h in range(2):
                 send(fsend.at[at, j, h], arecv.at[at, row], a_send.at[at], a_recv.at[at], (2 * col + j, chip * 2 + h))
 
+        if level == 1:
+            loads[3].wait()
+            loads[4].wait()
         if level + 1 < levels:
             early = [sum(fterm(level + 1, b, j) for b in range(level)) for j in range(2)]
 
@@ -175,12 +195,12 @@
             if level == levels - 1:
                 solve_and_spread(level, fbuf[level, core])
 
-            def along(i, _):
-                to = (col + i) % cols
-                remote(fbuf.at[level, core], fbuf.at[level, core], b_send.at[at], b_recv.at[at], (row, to)).start()
+            def along(n, _):
+                to = (row, col_at(n))
+                remote(fbuf.at[level, core], fbuf.at[level, core], b_send.at[at], b_recv.at[at], to).start()
                 return 0
 
-            lax.fori_loop(1, cols, along, 0)
+            lax.fori_loop(0, cols - 1, along, 0)
 
         if level + 1 < levels:
             await_halves(fbuf.at[level], b_recv.at[at])
@@ -193,33 +213,56 @@
         if early is not None:
             upper = upper + early
         usend[level] = upper.astype(BF16).reshape(2, half, width)
+        if level > 0:
+            for h in range(2):
+                to = (row, home_chip * 2 + h)
+                send(usend.at[level, h], rrecv.at[level, col], r_send.at[level], r_recv.at[level], to)
+            early = sum(bterm(later, level - 1, j) for later in range(level + 1, levels) for j in range(2))
+
+            @pl.when(at_home)
+            def _():
+                await_recv(rrecv.at[level], r_recv.at[level])
+                total = jnp.sum(rrecv[level].astype(F32), axis=0)
+                solve_and_spread(level, (fbuf[level, core].astype(F32) - total).astype(BF16))
+
+    def to_chips(n, _):
+        to_chip = (chip + around(n, 8)) % 8
         for h in range(2):
-            send(usend.at[level, h], rrecv.at[level, col], r_send.at[level], r_recv.at[level], (row, home_chip * 2 + h))
-        if level > 0:
-            early = sum(bterm(later, level - 1, j) for later in range(level + 1, levels) for j in range(2))
-
-        @pl.when(at_home)
-        def _():
-            await_recv(rrecv.at[level], r_recv.at[level])
-            total = jnp.sum(rrecv[level].astype(F32), axis=0)
-            solve_and_spread(level, (fbuf[level, core].astype(F32) - total).astype(BF16))
+            remote(usend.at[0, h], rrecv.at[0, col], r_send.at[0], r_recv.at[0], (row, to_chip * 2 + h)).start()
+        return 0
+
+    lax.fori_loop(0, cols // 2 - 1, to_chips, 0)
+    other = (row, chip * 2 + 1 - core)
+    remote(usend.at[0, 1 - core], rrecv.at[0, col], r_send.at[0], r_recv.at[0], other).start()
+    pltpu.make_async_copy(usend.at[0, core], rrecv.at[0, col], r_recv.at[0]).start()
 
     await_halves(fbuf.at[levels - 1], b_recv.at[levels - 2])
     forward_out[...] = fbuf[...].reshape(forward_out.shape)
-    for level in range(levels - 1, -1, -1):
+    for level in range(levels - 1, 0, -1):
         await_halves(sbuf.at[level], s_recv.at[level])
         solution_out[level] = both(sbuf.at[level])
 
+    await_recv(rrecv.at[0], r_recv.at[0])
+    total = jnp.sum(rrecv[0].astype(F32), axis=0)
+    zeta = (fbuf[0, core].astype(F32) - total).astype(BF16)
+    sbuf[0, core] = times(zeta, diag[0]).astype(BF16)
+    remote(sbuf.at[0, core], sbuf.at[0, core], s_send.at[0], s_recv.at[0], other).start()
+    await_recv(sbuf.at[0, 0], s_recv.at[0])
+    solution_out[0] = both(sbuf.at[0])
+
+    await_send(1, s_send.at[0])
+    await_send(cols - 1, r_send.at[0])
     for at in range(levels - 1):
 
         @pl.when(is_self)
         def _():
             await_send(3, a_send.at[at])
-            await_send(1, r_send.at[at])
 
         @pl.when(jnp.logical_not(is_self))
         def _():
             await_send(4, a_send.at[at])
+
+        if at > 0:
 
             @pl.when(at_home)
             def _():
@@ -243,7 +286,7 @@
 
     @pl.when(at_home)
     def _():
-        for level in range(levels):
+        for level in range(1, levels):
             await_send(cols - 1, s_send.at[level])
 
 
@@ -253,15 +296,18 @@
     rows, cols = lax.axis_size("row"), lax.axis_size("col")
     half = count // 2
     steps = levels - 1
-    vmem = pl.BlockSpec(memory_space=pltpu.VMEM)
+    vmem, hbm = pl.BlockSpec(memory_space=pltpu.VMEM), pl.BlockSpec(memory_space=pltpu.HBM)
     dma = pltpu.SemaphoreType.DMA
     out = jax.ShapeDtypeStruct((levels, count, width), BF16)
     forward, solved = pl.pallas_call(
         functools.partial(kernel, levels, rows, cols),
         out_shape=(out, out),
-        in_specs=[vmem, vmem, pl.BlockSpec(memory_space=pltpu.SMEM), vmem],
+        in_specs=[hbm, hbm, pl.BlockSpec(memory_space=pltpu.SMEM), hbm],
         out_specs=(vmem, vmem),
         scratch_shapes=[
+            pltpu.VMEM((levels, count, width), BF16),
+            pltpu.VMEM((pairs * block_rows, width, width), BF16),
+            pltpu.VMEM((levels, width, width), BF16),
             pltpu.VMEM((steps, 2, 2, half, width), BF16),
             pltpu.VMEM((steps, rows, half, width), BF16),
             pltpu.VMEM((levels, 2, half, width), BF16),
@@ -271,13 +317,13 @@
             pltpu.VMEM((levels, 2, 2, half, width), BF16),
         ]
         + [dma((steps,))] * 8
-        + [dma((levels,))] * 2,
-        compiler_params=pltpu.CompilerParams(collective_id=0, has_side_effects=True, vmem_limit_bytes=32 << 20),
+        + [dma((levels,))] * 3,
+        compiler_params=pltpu.CompilerParams(collective_id=0, has_side_effects=True),
         name="solves",
     )(
         rhs.reshape(levels, count, width),
         factor.reshape(pairs * block_rows, width, width),
-        pattern,
+        pattern.transpose(1, 2, 0),
         diag_inverse.reshape(levels, width, width),
     )
     return forward.reshape(rhs.shape), solved.reshape(rhs.shape)

time: 120 us -> 113 us (0.942)
  the two profiles are of different devices: /device:TPU:13 before, /device:TPU:1 now
where the time goes in v2:
time: 113 us
  Pallas kernels  109 us (96%)
  local copies, waits for them, and re-layouts  3.05 us (3%)
    pallas_call x1, Pallas kernels, on_device(): pl.pallas_call(functools.partial(kernel, levels, rows, cols), out_shape=(...  109 us
    unnamed x2, local copies, waits for them, and re-layouts  3.05 us

profile of v2, /device:TPU:1, one launch (start us, length us, event | category | flops | bytes accessed | tf_op | source)
XLA Modules:
  0.0 112.7 jit_solution(16846972125734970777)
XLA Ops:
  0.6 109.0 %solves.1 = (bf16[5,32,256]{2,1,0:T(8,128)(2,1)}, bf16[5,32,256]{2,1,0:T(8,128)(2,1)}) custom-call(bf16[5,32,256]{2,1,0:T(8,128)(2,1)} %bitcast.12, bf16[20,256,256]{2,1,0:T(8,128)(2,1)} %bitcast.10, s32[2,1,10]{2,1,0:T(1,128)} %bitcast.15, bf16[5,256,256]{2,1,0:T(8,128)(2,1)} %bitcast.11), custom_call_target="tpu_custom_call" | custom-call | tf_op jit(solution)/shard_map/solves/pallas_call | solution.py:302
  109.7 1.5 %copy.10 = bf16[5,1,32,256]{3,2,1,0:T(8,128)(2,1)} copy(bf16[5,1,32,256]{3,2,1,0:T(8,128)(2,1)} %bitcast.14) | data formatting | bytes 163840
  111.2 1.5 %copy.11 = bf16[5,1,32,256]{3,2,1,0:T(8,128)(2,1)} copy(bf16[5,1,32,256]{3,2,1,0:T(8,128)(2,1)} %bitcast.13) | data formatting | bytes 163840

commit v3 on v2

v3 whole, which is shorter than its diff:
```python
import functools

import jax
import jax.numpy as jnp
from jax import lax
from jax.experimental import pallas as pl
from jax.experimental.pallas import tpu as pltpu
from jax.sharding import PartitionSpec as P

MESH = pl.DeviceIdType.MESH
BF16 = jnp.bfloat16
F32 = jnp.float32


def pair_index(later, earlier):
    return later * (later - 1) // 2 + earlier


def times_transposed(left, right):
    return lax.dot_general(left, right, (((1,), (1,)), ((), ())), preferred_element_type=F32)


def times(left, right):
    return lax.dot_general(left, right, (((1,), (0,)), ((), ())), preferred_element_type=F32)


def kernel(
    levels, rows, cols,
    rhs_hbm, factor_hbm, pattern, diag_hbm, forward_out, solution_out,
    rhs, factor, diag, fsend, arecv, zbuf, ebuf, usend, rrecv, sq, sbuf, pbuf, usend0, rrecv0, sbuf0, stop, ptop,
    a_send, a_recv, b_send, b_recv, r_send, r_recv, p_send, p_recv, s_send, s_recv, loaded,
):
    row = lax.axis_index("row")
    col = lax.axis_index("col")
    core = col % 2
    chip = col // 2
    home_col = row // 2
    home_chip = home_col // 2
    at_home = chip == home_chip
    own_slot = row % 2
    is_self = at_home & (col == home_col)
    is_server = ((row // 4) % 2 == chip % 2) & ((row // 2) % 2 == core)
    served_row = chip // 2 * 8 + row % 8
    quarter = row // 8
    top = levels - 1
    half = fsend.shape[3]
    width = rhs.shape[-1]

    def remote(src, dst, send_sem, recv_sem, device):
        return pltpu.make_async_remote_copy(
            src_ref=src, dst_ref=dst, send_sem=send_sem, recv_sem=recv_sem, device_id=device, device_id_type=MESH
        )

    def send(src, dst, send_sem, recv_sem, device):
        same = (device[0] == row) & (device[1] == col)

        @pl.when(same)
        def _():
            pltpu.make_async_copy(src, dst, recv_sem).start()

        @pl.when(jnp.logical_not(same))
        def _():
            remote(src, dst, send_sem, recv_sem, device).start()

    def await_recv(ref, sem):
        remote(ref, ref, sem, sem, (row, col)).wait_recv()

    def await_sends(count, sem, slots):
        ref = slots.at[0, pl.ds(0, count)]
        remote(ref, ref, sem, sem, (row, col)).wait_send()

    pairs = [(later, earlier) for later in range(1, levels) for earlier in range(later)]
    loads = [
        pltpu.make_async_copy(src, dst, loaded.at[n])
        for n, (src, dst) in enumerate(
            [
                (rhs_hbm, rhs),
                (diag_hbm.at[0], diag.at[0]),
                (factor_hbm.at[pl.ds(0, 2)], factor.at[pl.ds(0, 2)]),
                (diag_hbm.at[pl.ds(1, levels - 1)], diag.at[pl.ds(1, levels - 1)]),
                (factor_hbm.at[pl.ds(2, factor.shape[0] - 2)], factor.at[pl.ds(2, factor.shape[0] - 2)]),
            ]
        )
    ]
    for load in loads:
        load.start()

    barrier = pltpu.get_barrier_semaphore()

    def greet(device):
        same = (device[0] == row) & (device[1] == col)

        @pl.when(jnp.logical_not(same))
        def _():
            pl.semaphore_signal(barrier, inc=1, device_id=device, device_id_type=MESH)

    def around(n, size):
        return (size // 2 + (1 - 2 * (n % 2)) * ((n + 1) // 2)) % size

    def row_at(n):
        return (row // 8 + around(n % 4, 4)) % 4 * 8 + (row + around(n // 4, 8)) % 8

    def col_at(n):
        return (chip + around(n // 2, 8)) % 8 * 2 + (core + 1 - n % 2) % 2

    def repeat(count, step):
        def body(n, _):
            step(n)
            return 0

        lax.fori_loop(0, count, body, 0)

    @pl.when(at_home)
    def _():
        repeat(rows, lambda n: greet((row_at(n), home_col)))

    for h in range(2):
        greet((row, home_chip * 2 + h))

    def fold(later, earlier):
        index = pair_index(later, earlier)

        def one(j):
            block = times(factor[2 * index + j], diag[earlier]) * pattern[j, 0, index].astype(F32)
            factor[2 * index + j] = block.astype(BF16)

        repeat(2, one)

    def joined(ref):
        return ref[...].reshape(2 * half, width)

    def zeta_of(level):
        return rhs[0] if level == 0 else joined(zbuf.at[level])

    def fterm(later, earlier, j):
        return times_transposed(zeta_of(earlier), factor[2 * pair_index(later, earlier) + j])

    def bterm(later, earlier, j):
        solved = joined(ptop.at[j] if later == top else pbuf.at[later, j])
        return times(solved, factor[2 * pair_index(later, earlier) + j])

    def finish_forward(level):
        solved = times_transposed(zeta_of(level), diag[level]).astype(BF16)
        forward_out[level] = solved
        ebuf[level] = times(solved, diag[level])

    def await_halves(buf, sem):
        @pl.when(at_home)
        def _():
            await_recv(buf.at[0], sem)

        @pl.when(jnp.logical_not(at_home))
        def _():
            await_recv(buf, sem)

    def to_column(src, dst, send_sem, recv_sem):
        repeat(cols - 1, lambda n: remote(src, dst, send_sem, recv_sem, (row, col_at(n))).start())

    for load in loads[:3]:
        load.wait()
    fold(1, 0)
    lower = [fterm(1, 0, j) for j in range(2)]

    for level in range(1, levels):
        at = level - 1
        for j in range(2):
            fsend[at, j] = lower[j].astype(BF16).reshape(2, half, width)
        if level == 1:

            @pl.when(jnp.logical_not(at_home))
            def _():
                pl.semaphore_wait(barrier, 4)

            @pl.when(at_home & jnp.logical_not(is_self))
            def _():
                pl.semaphore_wait(barrier, 4 + cols - 1)

            @pl.when(is_self)
            def _():
                pl.semaphore_wait(barrier, 3 + cols - 1)

        for j in range(2):
            for h in range(2):
                send(fsend.at[at, j, h], arecv.at[at, row], a_send.at[at], a_recv.at[at], (2 * col + j, chip * 2 + h))

        if level == 1:
            loads[3].wait()
            loads[4].wait()
            for later, earlier in pairs[1:]:
                fold(later, earlier)
        if level + 1 < levels:
            early = [sum(fterm(level + 1, b, j) for b in range(level)) for j in range(2)]
        finish_forward(level - 1)

        @pl.when(at_home)
        def _():
            await_recv(arecv.at[at], a_recv.at[at])
            total = jnp.sum(arecv[at].astype(F32), axis=0)
            zeta = (rhs[level, pl.ds(pl.multiple_of(core * half, half), half)].astype(F32) - total).astype(BF16)
            if level < top:
                zbuf[level, core] = zeta
            else:
                solved = times_transposed(zeta, diag[top]).astype(BF16)
                zbuf[top, core] = solved
                stop[core] = times(solved, diag[top]).astype(BF16)
                slot = ptop.at[own_slot, core]
                repeat(
                    rows - 1,
                    lambda n: remote(
                        stop.at[core], slot, p_send.at[top - 1], p_recv.at[top - 1], (row_at(n), home_col)
                    ).start(),
                )
                send(stop.at[core], slot, p_send.at[top - 1], p_recv.at[top - 1], (row, home_col))
                to_column(stop.at[core], stop.at[core], s_send.at[top], s_recv.at[top])
            to_column(zbuf.at[level, core], zbuf.at[level, core], b_send.at[at], b_recv.at[at])

        if level < top:
            await_halves(zbuf.at[level], b_recv.at[at])
            lower = [early[j] + fterm(level + 1, level, j) for j in range(2)]

    early = None
    for level in range(top - 1, -1, -1):
        await_recv(ptop if level + 1 == top else pbuf.at[level + 1], p_recv.at[level])
        upper = bterm(level + 1, level, 0) + bterm(level + 1, level, 1)
        if early is not None:
            upper = upper + early
        if level > 0:
            mine = jnp.where(col == home_col, ebuf[level] - upper, -upper)
            usend[level] = mine.astype(BF16).reshape(usend.shape[1:])
            for q in range(4):
                to = (q * 8 + row % 8, home_col)
                send(usend.at[level, q], rrecv.at[level, col], r_send.at[level], r_recv.at[level], to)
            early = sum(bterm(later, level - 1, j) for later in range(level + 1, levels) for j in range(2))

            @pl.when(is_server)
            def _():
                slots = rrecv.at[level, pl.ds(0, cols)]
                await_recv(slots, r_recv.at[level])
                sq[level] = jnp.sum(slots[...].astype(F32), axis=0).astype(BF16)
                at = level - 1

                def spread(n):
                    to = (row_at(n), col)
                    remote(sq.at[level], pbuf.at[level, own_slot, quarter], p_send.at[at], p_recv.at[at], to).start()

                repeat(rows - 1, spread)
                pltpu.make_async_copy(sq.at[level], pbuf.at[level, own_slot, quarter], p_recv.at[at]).start()

                def give(n):
                    to = (served_row, col_at(n))
                    remote(sq.at[level], sbuf.at[level, quarter], s_send.at[level], s_recv.at[level], to).start()

                repeat(cols - 1, give)
                to = (served_row, col)
                send(sq.at[level], sbuf.at[level, quarter], s_send.at[level], s_recv.at[level], to)

    usend0[...] = upper.astype(BF16).reshape(usend0.shape)

    def to_chips(n):
        to_chip = (chip + around(n, 8)) % 8
        for h in range(2):
            remote(usend0.at[h], rrecv0.at[0, col], r_send.at[0], r_recv.at[0], (row, to_chip * 2 + h)).start()

    repeat(cols // 2 - 1, to_chips)
    other = (row, chip * 2 + 1 - core)
    remote(usend0.at[1 - core], rrecv0.at[0, col], r_send.at[0], r_recv.at[0], other).start()
    pltpu.make_async_copy(usend0.at[core], rrecv0.at[0, col], r_recv.at[0]).start()

    await_halves(zbuf.at[top], b_recv.at[top - 1])
    forward_out[top] = joined(zbuf.at[top])
    await_halves(stop, s_recv.at[top])
    solution_out[top] = joined(stop)
    for level in range(top - 1, 0, -1):
        await_recv(sbuf.at[level], s_recv.at[level])
        solution_out[level] = joined(sbuf.at[level])

    await_recv(rrecv0.at[0], r_recv.at[0])
    total = jnp.sum(rrecv0[0].astype(F32), axis=0)
    mine = ebuf[0, pl.ds(pl.multiple_of(core * half, half), half)]
    sbuf0[core] = (mine - total).astype(BF16)
    remote(sbuf0.at[core], sbuf0.at[core], s_send.at[0], s_recv.at[0], other).start()
    await_recv(sbuf0.at[0], s_recv.at[0])
    solution_out[0] = joined(sbuf0)

    await_sends(1, s_send.at[0], rrecv0)
    await_sends(cols - 1, r_send.at[0], rrecv0)
    for at in range(top):

        @pl.when(is_self)
        def _():
            await_sends(3, a_send.at[at], arecv)

        @pl.when(jnp.logical_not(is_self))
        def _():
            await_sends(4, a_send.at[at], arecv)

        @pl.when(at_home)
        def _():
            await_sends(cols - 1, b_send.at[at], arecv)

    @pl.when(at_home)
    def _():
        await_sends(cols - 1, s_send.at[top], arecv)

        @pl.when(is_self)
        def _():
            await_sends(rows - 1, p_send.at[top - 1], arecv)

        @pl.when(jnp.logical_not(is_self))
        def _():
            await_sends(rows, p_send.at[top - 1], arecv)

    for level in range(1, top):

        @pl.when(is_self)
        def _():
            await_sends(3, r_send.at[level], rrecv)
            await_sends(cols - 1, s_send.at[level], rrecv)

        @pl.when(jnp.logical_not(is_self))
        def _():
            await_sends(4, r_send.at[level], rrecv)

        @pl.when(is_server)
        def _():
            await_sends(rows - 1, p_send.at[level - 1], rrecv)

        @pl.when(is_server & jnp.logical_not(is_self))
        def _():
            await_sends(cols, s_send.at[level], rrecv)


def on_device(rhs, factor, pattern, diag_inverse):
    levels, _, count, width = rhs.shape
    pairs, block_rows = factor.shape[:2]
    rows, cols = lax.axis_size("row"), lax.axis_size("col")
    half = count // 2
    steps = levels - 1
    vmem, hbm = pl.BlockSpec(memory_space=pltpu.VMEM), pl.BlockSpec(memory_space=pltpu.HBM)
    dma = pltpu.SemaphoreType.DMA
    out = pltpu.VMEM((levels, count, width), BF16)
    forward, solved = pl.pallas_call(
        functools.partial(kernel, levels, rows, cols),
        out_shape=(out, out),
        in_specs=[hbm, hbm, pl.BlockSpec(memory_space=pltpu.SMEM), hbm],
        out_specs=(vmem, vmem),
        scratch_shapes=[
            pltpu.VMEM((levels, count, width), BF16),
            pltpu.VMEM((pairs * block_rows, width, width), BF16),
            pltpu.VMEM((levels, width, width), BF16),
            pltpu.VMEM((steps, 2, 2, half, width), BF16),
            pltpu.VMEM((steps, rows, half, width), BF16),
            pltpu.VMEM((levels, 2, half, width), BF16),
            pltpu.VMEM((steps, count, width), F32),
            pltpu.VMEM((steps, 4, half // 2, width), BF16),
            pltpu.VMEM((steps, rows, half // 2, width), BF16),
            pltpu.VMEM((steps, half // 2, width), BF16),
            pltpu.VMEM((steps, 4, half // 2, width), BF16),
            pltpu.VMEM((steps, 2, 4, half // 2, width), BF16),
            pltpu.VMEM((2, half, width), BF16),
            pltpu.VMEM((1, cols, half, width), BF16),
            pltpu.VMEM((2, half, width), BF16),
            pltpu.VMEM((2, half, width), BF16),
            pltpu.VMEM((2, 2, half, width), BF16),
        ]
        + [dma((steps,))] * 8
        + [dma((levels,))] * 3,
        compiler_params=pltpu.CompilerParams(collective_id=0, has_side_effects=True),
        name="solves",
    )(
        rhs.reshape(levels, count, width),
        factor.reshape(pairs * block_rows, width, width),
        pattern.transpose(1, 2, 0),
        diag_inverse.reshape(levels, width, width),
    )
    return forward.reshape(rhs.shape), solved.reshape(rhs.shape)


def solution(mesh):
    return jax.shard_map(
        on_device,
        mesh=mesh,
        in_specs=(
            P(None, "row", None, None),
            P(None, "col", "row", None, None),
            P(None, "col", "row"),
            P(None, "row", None, None),
        ),
        out_specs=(P(None, "row", None, None), P(None, "row", None, None)),
        check_vma=False,
    )
```

time: 113 us -> 104 us (0.920)
  Pallas kernels: 109 us -> 102 us
  local copies, waits for them, and re-layouts: 3.05 us -> 1.27 us
    pallas_call x1, Pallas kernels: 109 us -> 102 us  [on_device(): pl.pallas_call(functools.partial(kernel, levels, rows, cols), out_shape=(...]
    unnamed x2, local copies, waits for them, and re-layouts: 3.05 us -> 1.27 us
where the time goes in v3:
time: 104 us
  Pallas kernels  102 us (98%)
  local copies, waits for them, and re-layouts  1.27 us (1%)
    pallas_call x1, Pallas kernels, on_device(): pl.pallas_call(functools.partial(kernel, levels, rows, cols), out_shape=(...  102 us

profile of v3, /device:TPU:1, one launch (start us, length us, event | category | flops | bytes accessed | tf_op | source)
XLA Modules:
  0.0 104.2 jit_solution(1193346881977942770)
XLA Ops:
  0.6 102.3 %solves.1 = (bf16[5,32,256]{2,1,0:T(8,128)(2,1)S(1)}, bf16[5,32,256]{2,1,0:T(8,128)(2,1)S(1)}) custom-call(bf16[5,32,256]{2,1,0:T(8,128)(2,1)} %bitcast.14, bf16[20,256,256]{2,1,0:T(8,128)(2,1)} %bitcast.12, s32[2,1,10]{2,1,0:T(1,128)} %bitcast.15, bf16[5,256,256]{2,1,0:T(8,128)(2,1)} %bitcast.13), custom_call_target="tpu_custom_call" | custom-call | tf_op jit(solution)/shard_map/solves/pallas_call | solution.py:342
  103.0 0.6 copy.10
  103.6 0.6 copy.11

commit v4 on v3

--- a/solution.py
+++ b/solution.py
@@ -27,8 +27,9 @@
 def kernel(
     levels, rows, cols,
     rhs_hbm, factor_hbm, pattern, diag_hbm, forward_out, solution_out,
-    rhs, factor, diag, fsend, arecv, zbuf, ebuf, usend, rrecv, sq, sbuf, pbuf, usend0, rrecv0, sbuf0, stop, ptop,
-    a_send, a_recv, b_send, b_recv, r_send, r_recv, p_send, p_recv, s_send, s_recv, loaded,
+    rhs, factor, diag, dtop, fsend, arecv, zbuf, ebuf, ftop_send, atop, fq, ftop, usend, rrecv, sq, sbuf, pbuf,
+    usend0, rrecv0, sbuf0,
+    a_send, a_recv, b_send, b_recv, r_send, r_recv, p_send, p_recv, s_send, s_recv, loaded, d_send, d_recv,
 ):
     row = lax.axis_index("row")
     col = lax.axis_index("col")
@@ -136,8 +137,7 @@
         return times_transposed(zeta_of(earlier), factor[2 * pair_index(later, earlier) + j])
 
     def bterm(later, earlier, j):
-        solved = joined(ptop.at[j] if later == top else pbuf.at[later, j])
-        return times(solved, factor[2 * pair_index(later, earlier) + j])
+        return times(joined(pbuf.at[later, j]), factor[2 * pair_index(later, earlier) + j])
 
     def finish_forward(level):
         solved = times_transposed(zeta_of(level), diag[level]).astype(BF16)
@@ -153,15 +153,27 @@
         def _():
             await_recv(buf, sem)
 
-    def to_column(src, dst, send_sem, recv_sem):
-        repeat(cols - 1, lambda n: remote(src, dst, send_sem, recv_sem, (row, col_at(n))).start())
+    def serve(level):
+        at = level - 1
+
+        def spread(n):
+            to = (row_at(n), col)
+            remote(sq.at[level], pbuf.at[level, own_slot, quarter], p_send.at[at], p_recv.at[at], to).start()
+
+        repeat(rows - 1, spread)
+        pltpu.make_async_copy(sq.at[level], pbuf.at[level, own_slot, quarter], p_recv.at[at]).start()
+        give(sq.at[level], sbuf.at[level, quarter], s_send.at[level], s_recv.at[level])
+
+    def give(src, dst, send_sem, recv_sem):
+        repeat(cols - 1, lambda n: remote(src, dst, send_sem, recv_sem, (served_row, col_at(n))).start())
+        send(src, dst, send_sem, recv_sem, (served_row, col))
 
     for load in loads[:3]:
         load.wait()
     fold(1, 0)
     lower = [fterm(1, 0, j) for j in range(2)]
 
-    for level in range(1, levels):
+    for level in range(1, top):
         at = level - 1
         for j in range(2):
             fsend[at, j] = lower[j].astype(BF16).reshape(2, half, width)
@@ -188,39 +200,50 @@
             loads[4].wait()
             for later, earlier in pairs[1:]:
                 fold(later, earlier)
-        if level + 1 < levels:
-            early = [sum(fterm(level + 1, b, j) for b in range(level)) for j in range(2)]
+        early = [sum(fterm(level + 1, b, j) for b in range(level)) for j in range(2)]
         finish_forward(level - 1)
 
         @pl.when(at_home)
         def _():
             await_recv(arecv.at[at], a_recv.at[at])
             total = jnp.sum(arecv[at].astype(F32), axis=0)
-            zeta = (rhs[level, pl.ds(pl.multiple_of(core * half, half), half)].astype(F32) - total).astype(BF16)
-            if level < top:
-                zbuf[level, core] = zeta
-            else:
-                solved = times_transposed(zeta, diag[top]).astype(BF16)
-                zbuf[top, core] = solved
-                stop[core] = times(solved, diag[top]).astype(BF16)
-                slot = ptop.at[own_slot, core]
-                repeat(
-                    rows - 1,
-                    lambda n: remote(
-                        stop.at[core], slot, p_send.at[top - 1], p_recv.at[top - 1], (row_at(n), home_col)
-                    ).start(),
-                )
-                send(stop.at[core], slot, p_send.at[top - 1], p_recv.at[top - 1], (row, home_col))
-                to_column(stop.at[core], stop.at[core], s_send.at[top], s_recv.at[top])
-            to_column(zbuf.at[level, core], zbuf.at[level, core], b_send.at[at], b_recv.at[at])
-
-        if level < top:
-            await_halves(zbuf.at[level], b_recv.at[at])
-            lower = [early[j] + fterm(level + 1, level, j) for j in range(2)]
+            own_half = rhs[level, pl.ds(pl.multiple_of(core * half, half), half)].astype(F32)
+            zbuf[level, core] = (own_half - total).astype(BF16)
+            own = zbuf.at[level, core]
+            repeat(cols - 1, lambda n: remote(own, own, b_send.at[at], b_recv.at[at], (row, col_at(n))).start())
+
+        await_halves(zbuf.at[level], b_recv.at[at])
+        lower = [early[j] + fterm(level + 1, level, j) for j in range(2)]
+        if level == 1:
+
+            @pl.when(is_self)
+            def _():
+                for q in range(4):
+                    send(diag.at[top], dtop, d_send, d_recv, (q * 8 + row % 8, home_col))
+
+    at = top - 1
+    for j in range(2):
+        mine = jnp.where(is_self & (own_slot == j), rhs[top].astype(F32) - lower[j], -lower[j])
+        ftop_send[j] = mine.astype(BF16).reshape(ftop_send.shape[1:])
+    for j in range(2):
+        for q in range(4):
+            to = (q * 8 + (2 * col + j) % 8, col)
+            send(ftop_send.at[j, q], atop.at[row], a_send.at[at], a_recv.at[at], to)
+    finish_forward(top - 1)
+
+    @pl.when(is_server)
+    def _():
+        await_recv(dtop, d_recv)
+        await_recv(atop, a_recv.at[at])
+        zeta = jnp.sum(atop[...].astype(F32), axis=0).astype(BF16)
+        fq[...] = times_transposed(zeta, dtop[...]).astype(BF16)
+        sq[top] = times(fq[...], dtop[...]).astype(BF16)
+        serve(top)
+        give(fq, ftop.at[quarter], b_send.at[at], b_recv.at[at])
 
     early = None
     for level in range(top - 1, -1, -1):
-        await_recv(ptop if level + 1 == top else pbuf.at[level + 1], p_recv.at[level])
+        await_recv(pbuf.at[level + 1], p_recv.at[level])
         upper = bterm(level + 1, level, 0) + bterm(level + 1, level, 1)
         if early is not None:
             upper = upper + early
@@ -237,22 +260,7 @@
                 slots = rrecv.at[level, pl.ds(0, cols)]
                 await_recv(slots, r_recv.at[level])
                 sq[level] = jnp.sum(slots[...].astype(F32), axis=0).astype(BF16)
-                at = level - 1
-
-                def spread(n):
-                    to = (row_at(n), col)
-                    remote(sq.at[level], pbuf.at[level, own_slot, quarter], p_send.at[at], p_recv.at[at], to).start()
-
-                repeat(rows - 1, spread)
-                pltpu.make_async_copy(sq.at[level], pbuf.at[level, own_slot, quarter], p_recv.at[at]).start()
-
-                def give(n):
-                    to = (served_row, col_at(n))
-                    remote(sq.at[level], sbuf.at[level, quarter], s_send.at[level], s_recv.at[level], to).start()
-
-                repeat(cols - 1, give)
-                to = (served_row, col)
-                send(sq.at[level], sbuf.at[level, quarter], s_send.at[level], s_recv.at[level], to)
+                serve(level)
 
     usend0[...] = upper.astype(BF16).reshape(usend0.shape)
 
@@ -266,11 +274,9 @@
     remote(usend0.at[1 - core], rrecv0.at[0, col], r_send.at[0], r_recv.at[0], other).start()
     pltpu.make_async_copy(usend0.at[core], rrecv0.at[0, col], r_recv.at[0]).start()
 
-    await_halves(zbuf.at[top], b_recv.at[top - 1])
-    forward_out[top] = joined(zbuf.at[top])
-    await_halves(stop, s_recv.at[top])
-    solution_out[top] = joined(stop)
-    for level in range(top - 1, 0, -1):
+    await_recv(ftop, b_recv.at[top - 1])
+    forward_out[top] = joined(ftop)
+    for level in range(top, 0, -1):
         await_recv(sbuf.at[level], s_recv.at[level])
         solution_out[level] = joined(sbuf.at[level])
 
@@ -284,50 +290,43 @@
 
     await_sends(1, s_send.at[0], rrecv0)
     await_sends(cols - 1, r_send.at[0], rrecv0)
-    for at in range(top):
-
-        @pl.when(is_self)
-        def _():
-            await_sends(3, a_send.at[at], arecv)
-
-        @pl.when(jnp.logical_not(is_self))
-        def _():
-            await_sends(4, a_send.at[at], arecv)
-
-        @pl.when(at_home)
-        def _():
-            await_sends(cols - 1, b_send.at[at], arecv)
+    def await_all_but(one_less, count, sem, slots):
+        pl.when(one_less)(lambda: await_sends(count - 1, sem, slots))
+        pl.when(jnp.logical_not(one_less))(lambda: await_sends(count, sem, slots))
+
+    for at in range(top - 1):
+        await_all_but(is_self, 4, a_send.at[at], arecv)
+    await_all_but(is_server, 8, a_send.at[top - 1], rrecv)
+    for level in range(1, top):
+        await_all_but(is_self, 4, r_send.at[level], rrecv)
 
     @pl.when(at_home)
     def _():
-        await_sends(cols - 1, s_send.at[top], arecv)
-
-        @pl.when(is_self)
-        def _():
-            await_sends(rows - 1, p_send.at[top - 1], arecv)
-
-        @pl.when(jnp.logical_not(is_self))
-        def _():
-            await_sends(rows, p_send.at[top - 1], arecv)
-
-    for level in range(1, top):
-
-        @pl.when(is_self)
-        def _():
-            await_sends(3, r_send.at[level], rrecv)
-            await_sends(cols - 1, s_send.at[level], rrecv)
-
-        @pl.when(jnp.logical_not(is_self))
-        def _():
-            await_sends(4, r_send.at[level], rrecv)
-
-        @pl.when(is_server)
-        def _():
+        for at in range(top - 1):
+            await_sends(cols - 1, b_send.at[at], arecv)
+
+    @pl.when(is_server)
+    def _():
+        await_all_but(is_self, cols, b_send.at[top - 1], rrecv)
+        for level in range(1, levels):
+            await_all_but(is_self, cols, s_send.at[level], rrecv)
             await_sends(rows - 1, p_send.at[level - 1], rrecv)
 
-        @pl.when(is_server & jnp.logical_not(is_self))
-        def _():
-            await_sends(cols, s_send.at[level], rrecv)
+    @pl.when(is_self)
+    def _():
+        three = factor.at[pl.ds(0, 3)]
+        remote(three, three, d_send, d_send, (row, col)).wait_send()
+
+
+def copy_out(forward, solved, forward_out, solution_out, sems):
+    copies = [
+        pltpu.make_async_copy(forward, forward_out, sems.at[0]),
+        pltpu.make_async_copy(solved, solution_out, sems.at[1]),
+    ]
+    for copy in copies:
+        copy.start()
+    for copy in copies:
+        copy.wait()
 
 
 def on_device(rhs, factor, pattern, diag_inverse):
@@ -348,23 +347,27 @@
             pltpu.VMEM((levels, count, width), BF16),
             pltpu.VMEM((pairs * block_rows, width, width), BF16),
             pltpu.VMEM((levels, width, width), BF16),
-            pltpu.VMEM((steps, 2, 2, half, width), BF16),
-            pltpu.VMEM((steps, rows, half, width), BF16),
-            pltpu.VMEM((levels, 2, half, width), BF16),
+            pltpu.VMEM((width, width), BF16),
+            pltpu.VMEM((steps - 1, 2, 2, half, width), BF16),
+            pltpu.VMEM((steps - 1, rows, half, width), BF16),
+            pltpu.VMEM((steps, 2, half, width), BF16),
             pltpu.VMEM((steps, count, width), F32),
+            pltpu.VMEM((2, 4, half // 2, width), BF16),
+            pltpu.VMEM((rows, half // 2, width), BF16),
+            pltpu.VMEM((half // 2, width), BF16),
+            pltpu.VMEM((4, half // 2, width), BF16),
             pltpu.VMEM((steps, 4, half // 2, width), BF16),
             pltpu.VMEM((steps, rows, half // 2, width), BF16),
-            pltpu.VMEM((steps, half // 2, width), BF16),
-            pltpu.VMEM((steps, 4, half // 2, width), BF16),
-            pltpu.VMEM((steps, 2, 4, half // 2, width), BF16),
+            pltpu.VMEM((levels, half // 2, width), BF16),
+            pltpu.VMEM((levels, 4, half // 2, width), BF16),
+            pltpu.VMEM((levels, 2, 4, half // 2, width), BF16),
             pltpu.VMEM((2, half, width), BF16),
             pltpu.VMEM((1, cols, half, width), BF16),
             pltpu.VMEM((2, half, width), BF16),
-            pltpu.VMEM((2, half, width), BF16),
-            pltpu.VMEM((2, 2, half, width), BF16),
         ]
         + [dma((steps,))] * 8
-        + [dma((levels,))] * 3,
+        + [dma((levels,))] * 3
+        + [dma] * 2,
         compiler_params=pltpu.CompilerParams(collective_id=0, has_side_effects=True),
         name="solves",
     )(
@@ -373,6 +376,16 @@
         pattern.transpose(1, 2, 0),
         diag_inverse.reshape(levels, width, width),
     )
+    out = jax.ShapeDtypeStruct((levels, count, width), BF16)
+    forward, solved = pl.pallas_call(
+        copy_out,
+        out_shape=(out, out),
+        in_specs=[vmem, vmem],
+        out_specs=(hbm, hbm),
+        scratch_shapes=[dma((2,))],
+        compiler_params=pltpu.CompilerParams(vmem_limit_bytes=1 << 20),
+        name="results",
+    )(forward, solved)
     return forward.reshape(rhs.shape), solved.reshape(rhs.shape)
 
 

time: 104 us -> 102 us (0.981)
  local copies, waits for them, and re-layouts: 1.27 us -> 0 us
    pallas_call x1, Pallas kernels: 102 us -> 100 us  [on_device(): pl.pallas_call(functools.partial(kernel, levels, rows, cols), out_shape=(...]
    unnamed x2 -> x0, local copies, waits for them, and re-layouts: 1.27 us -> none
where the time goes in v4:
time: 102 us
  Pallas kernels  101 us (99%)
    pallas_call x1, Pallas kernels, on_device(): pl.pallas_call(functools.partial(kernel, levels, rows, cols), out_shape=(...  100 us

profile of v4, /device:TPU:1, one launch (start us, length us, event | category | flops | bytes accessed | tf_op | source)
XLA Modules:
  0.0 101.5 jit_solution(6070176686394617925)
XLA Ops:
  0.6 100.2 %solves.1 = (bf16[5,32,256]{2,1,0:T(8,128)(2,1)S(1)}, bf16[5,32,256]{2,1,0:T(8,128)(2,1)S(1)}) custom-call(bf16[5,32,256]{2,1,0:T(8,128)(2,1)} %bitcast.12, bf16[20,256,256]{2,1,0:T(8,128)(2,1)} %bitcast.10, s32[2,1,10]{2,1,0:T(1,128)} %bitcast.13, bf16[5,256,256]{2,1,0:T(8,128)(2,1)} %bitcast.11), custom_call_target="tpu_custom_call" | custom-call | tf_op jit(solution)/shard_map/solves/pallas_call | solution.py:341
  100.8 0.7 results.1

commit v5 on v4

--- a/solution.py
+++ b/solution.py
@@ -26,8 +26,8 @@
 
 def kernel(
     levels, rows, cols,
-    rhs_hbm, factor_hbm, pattern, diag_hbm, forward_out, solution_out,
-    rhs, factor, diag, dtop, fsend, arecv, zbuf, ebuf, ftop_send, atop, fq, ftop, usend, rrecv, sq, sbuf, pbuf,
+    rhs_hbm, factor_hbm, pattern_hbm, diag_hbm, forward_out, solution_out,
+    rhs, factor, pattern, diag, dtop, fsend, arecv, zbuf, ebuf, ftop_send, atop, fq, ftop, usend, rrecv, sq, sbuf, pbuf,
     usend0, rrecv0, sbuf0,
     a_send, a_recv, b_send, b_recv, r_send, r_recv, p_send, p_recv, s_send, s_recv, loaded, d_send, d_recv,
 ):
@@ -76,6 +76,7 @@
         for n, (src, dst) in enumerate(
             [
                 (rhs_hbm, rhs),
+                (pattern_hbm, pattern),
                 (diag_hbm.at[0], diag.at[0]),
                 (factor_hbm.at[pl.ds(0, 2)], factor.at[pl.ds(0, 2)]),
                 (diag_hbm.at[pl.ds(1, levels - 1)], diag.at[pl.ds(1, levels - 1)]),
@@ -95,14 +96,23 @@
         def _():
             pl.semaphore_signal(barrier, inc=1, device_id=device, device_id_type=MESH)
 
-    def around(n, size):
-        return (size // 2 + (1 - 2 * (n % 2)) * ((n + 1) // 2)) % size
-
-    def row_at(n):
-        return (row // 8 + around(n % 4, 4)) % 4 * 8 + (row + around(n // 4, 8)) % 8
-
-    def col_at(n):
-        return (chip + around(n // 2, 8)) % 8 * 2 + (core + 1 - n % 2) % 2
+    def ring(step, size):
+        return min(step, size - step)
+
+    def nearest_last(steps):
+        return sorted(steps, key=lambda s: -ring(s[0], 4) - ring(s[1], 8) - ring(s[2], 8) - s[3] / 2)
+
+    row_steps = nearest_last([(x, y, 0, 0) for x in range(4) for y in range(8)])
+    col_steps = nearest_last([(0, 0, z, k) for z in range(cols // 2) for k in range(2)])
+    row_by_x = [(quarter + x) % 4 * 8 for x in range(4)]
+    row_by_y = [(row + y) % 8 for y in range(8)]
+    col_by_z = [(chip + z) % (cols // 2) * 2 for z in range(cols // 2)]
+    col_by_core = [core, 1 - core]
+    plane = [row_by_x[x] + row_by_y[y] for x, y, _, _ in row_steps]
+    column = [col_by_z[z] + col_by_core[k] for _, _, z, k in col_steps]
+
+    first_rows = sorted(range(rows), key=lambda r: ring(r // 8, 4) + ring(r % 8, 8))
+    chips = cols // 2
 
     def repeat(count, step):
         def body(n, _):
@@ -113,7 +123,9 @@
 
     @pl.when(at_home)
     def _():
-        repeat(rows, lambda n: greet((row_at(n), home_col)))
+        for to_row in plane[:-1]:
+            pl.semaphore_signal(barrier, inc=1, device_id=(to_row, home_col), device_id_type=MESH)
+        greet((row, home_col))
 
     for h in range(2):
         greet((row, home_chip * 2 + h))
@@ -155,20 +167,22 @@
 
     def serve(level):
         at = level - 1
-
-        def spread(n):
-            to = (row_at(n), col)
-            remote(sq.at[level], pbuf.at[level, own_slot, quarter], p_send.at[at], p_recv.at[at], to).start()
-
-        repeat(rows - 1, spread)
-        pltpu.make_async_copy(sq.at[level], pbuf.at[level, own_slot, quarter], p_recv.at[at]).start()
-        give(sq.at[level], sbuf.at[level, quarter], s_send.at[level], s_recv.at[level])
+        solved, slot = sq.at[level], pbuf.at[level, own_slot, quarter]
+        if level > 1:
+            for to_row in plane[:-1]:
+                remote(solved, slot, p_send.at[at], p_recv.at[at], (to_row, col)).start()
+            pltpu.make_async_copy(solved, slot, p_recv.at[at]).start()
+        else:
+            for to_row in first_rows:
+                send(solved, slot, p_send.at[at], p_recv.at[at], (to_row, col))
+        give(solved, sbuf.at[level, quarter], s_send.at[level], s_recv.at[level])
 
     def give(src, dst, send_sem, recv_sem):
-        repeat(cols - 1, lambda n: remote(src, dst, send_sem, recv_sem, (served_row, col_at(n))).start())
+        for to_col in column[:-1]:
+            remote(src, dst, send_sem, recv_sem, (served_row, to_col)).start()
         send(src, dst, send_sem, recv_sem, (served_row, col))
 
-    for load in loads[:3]:
+    for load in loads[:4]:
         load.wait()
     fold(1, 0)
     lower = [fterm(1, 0, j) for j in range(2)]
@@ -196,8 +210,8 @@
                 send(fsend.at[at, j, h], arecv.at[at, row], a_send.at[at], a_recv.at[at], (2 * col + j, chip * 2 + h))
 
         if level == 1:
-            loads[3].wait()
             loads[4].wait()
+            loads[5].wait()
             for later, earlier in pairs[1:]:
                 fold(later, earlier)
         early = [sum(fterm(level + 1, b, j) for b in range(level)) for j in range(2)]
@@ -210,7 +224,8 @@
             own_half = rhs[level, pl.ds(pl.multiple_of(core * half, half), half)].astype(F32)
             zbuf[level, core] = (own_half - total).astype(BF16)
             own = zbuf.at[level, core]
-            repeat(cols - 1, lambda n: remote(own, own, b_send.at[at], b_recv.at[at], (row, col_at(n))).start())
+            for to_col in column[:-1]:
+                remote(own, own, b_send.at[at], b_recv.at[at], (row, to_col)).start()
 
         await_halves(zbuf.at[level], b_recv.at[at])
         lower = [early[j] + fterm(level + 1, level, j) for j in range(2)]
@@ -263,16 +278,11 @@
                 serve(level)
 
     usend0[...] = upper.astype(BF16).reshape(usend0.shape)
-
-    def to_chips(n):
-        to_chip = (chip + around(n, 8)) % 8
-        for h in range(2):
-            remote(usend0.at[h], rrecv0.at[0, col], r_send.at[0], r_recv.at[0], (row, to_chip * 2 + h)).start()
-
-    repeat(cols // 2 - 1, to_chips)
-    other = (row, chip * 2 + 1 - core)
-    remote(usend0.at[1 - core], rrecv0.at[0, col], r_send.at[0], r_recv.at[0], other).start()
-    pltpu.make_async_copy(usend0.at[core], rrecv0.at[0, col], r_recv.at[0]).start()
+    for z in range(chips):
+        for k in range(2):
+            for h in range(2) if z < 1 else [k]:
+                send(usend0.at[h], rrecv0.at[h, col], r_send.at[0], r_recv.at[0], (row, z * 2 + k))
+    starts_first = chip < 1
 
     await_recv(ftop, b_recv.at[top - 1])
     forward_out[top] = joined(ftop)
@@ -280,16 +290,26 @@
         await_recv(sbuf.at[level], s_recv.at[level])
         solution_out[level] = joined(sbuf.at[level])
 
-    await_recv(rrecv0.at[0], r_recv.at[0])
-    total = jnp.sum(rrecv0[0].astype(F32), axis=0)
-    mine = ebuf[0, pl.ds(pl.multiple_of(core * half, half), half)]
-    sbuf0[core] = (mine - total).astype(BF16)
-    remote(sbuf0.at[core], sbuf0.at[core], s_send.at[0], s_recv.at[0], other).start()
-    await_recv(sbuf0.at[0], s_recv.at[0])
-    solution_out[0] = joined(sbuf0)
-
-    await_sends(1, s_send.at[0], rrecv0)
-    await_sends(cols - 1, r_send.at[0], rrecv0)
+    @pl.when(starts_first)
+    def _():
+        await_recv(rrecv0, r_recv.at[0])
+        total = jnp.sum(rrecv0[...].astype(F32), axis=1).reshape(2 * half, width)
+        solution_out[0] = (ebuf[0] - total).astype(BF16)
+        await_sends(cols + 2 - 2, r_send.at[0], arecv)
+
+    @pl.when(jnp.logical_not(starts_first))
+    def _():
+        await_recv(rrecv0.at[core], r_recv.at[0])
+        total = jnp.sum(rrecv0[core].astype(F32), axis=0)
+        mine = ebuf[0, pl.ds(pl.multiple_of(core * half, half), half)]
+        sbuf0[core] = (mine - total).astype(BF16)
+        other = (row, chip * 2 + 1 - core)
+        remote(sbuf0.at[core], sbuf0.at[core], s_send.at[0], s_recv.at[0], other).start()
+        await_recv(sbuf0.at[0], s_recv.at[0])
+        solution_out[0] = joined(sbuf0)
+        await_sends(1, s_send.at[0], arecv)
+        await_sends(cols + 2 - 1, r_send.at[0], arecv)
+
     def await_all_but(one_less, count, sem, slots):
         pl.when(one_less)(lambda: await_sends(count - 1, sem, slots))
         pl.when(jnp.logical_not(one_less))(lambda: await_sends(count, sem, slots))
@@ -341,11 +361,12 @@
     forward, solved = pl.pallas_call(
         functools.partial(kernel, levels, rows, cols),
         out_shape=(out, out),
-        in_specs=[hbm, hbm, pl.BlockSpec(memory_space=pltpu.SMEM), hbm],
+        in_specs=[hbm, hbm, hbm, hbm],
         out_specs=(vmem, vmem),
         scratch_shapes=[
             pltpu.VMEM((levels, count, width), BF16),
             pltpu.VMEM((pairs * block_rows, width, width), BF16),
+            pltpu.SMEM((block_rows, 1, pairs), jnp.int32),
             pltpu.VMEM((levels, width, width), BF16),
             pltpu.VMEM((width, width), BF16),
             pltpu.VMEM((steps - 1, 2, 2, half, width), BF16),
@@ -362,11 +383,12 @@
             pltpu.VMEM((levels, 4, half // 2, width), BF16),
             pltpu.VMEM((levels, 2, 4, half // 2, width), BF16),
             pltpu.VMEM((2, half, width), BF16),
-            pltpu.VMEM((1, cols, half, width), BF16),
+            pltpu.VMEM((2, cols, half, width), BF16),
             pltpu.VMEM((2, half, width), BF16),
         ]
         + [dma((steps,))] * 8
-        + [dma((levels,))] * 3
+        + [dma((levels,))] * 2
+        + [dma((6,))]
         + [dma] * 2,
         compiler_params=pltpu.CompilerParams(collective_id=0, has_side_effects=True),
         name="solves",

time: 102 us -> 98.8 us (0.969)
  Pallas kernels: 101 us -> 98.1 us
    pallas_call x1, Pallas kernels: 100 us -> 97.4 us  [on_device(): pl.pallas_call(functools.partial(kernel, levels, rows, cols), out_shape=(...]
where the time goes in v5:
time: 98.8 us; the launch traced here: 98.7 us
  Pallas kernels  98.1 us (99%)
    pallas_call x1, Pallas kernels, on_device(): pl.pallas_call(functools.partial(kernel, levels, rows, cols), out_shape=(...  97.4 us

profile of v5, /device:TPU:1, one launch (start us, length us, event | category | flops | bytes accessed | tf_op | source)
XLA Modules:
  0.0 98.7 jit_solution(11670565404633728671)
XLA Ops:
  0.6 97.4 %solves.1 = (bf16[5,32,256]{2,1,0:T(8,128)(2,1)S(1)}, bf16[5,32,256]{2,1,0:T(8,128)(2,1)S(1)}) custom-call(bf16[5,32,256]{2,1,0:T(8,128)(2,1)} %bitcast.12, bf16[20,256,256]{2,1,0:T(8,128)(2,1)} %bitcast.10, s32[2,1,10]{2,1,0:T(1,128)} %bitcast.13, bf16[5,256,256]{2,1,0:T(8,128)(2,1)} %bitcast.11), custom_call_target="tpu_custom_call" | custom-call | tf_op jit(solution)/shard_map/solves/pallas_call | solution.py:361
  98.0 0.7 results.1

commit v6 on v5

--- a/solution.py
+++ b/solution.py
@@ -29,7 +29,7 @@
     rhs_hbm, factor_hbm, pattern_hbm, diag_hbm, forward_out, solution_out,
     rhs, factor, pattern, diag, dtop, fsend, arecv, zbuf, ebuf, ftop_send, atop, fq, ftop, usend, rrecv, sq, sbuf, pbuf,
     usend0, rrecv0, sbuf0,
-    a_send, a_recv, b_send, b_recv, r_send, r_recv, p_send, p_recv, s_send, s_recv, loaded, d_send, d_recv,
+    a_send, a_recv, b_send, b_recv, r_send, r_recv, p_send, p_recv, s_send, s_recv, loaded, d_send, d_recv, ready,
 ):
     row = lax.axis_index("row")
     col = lax.axis_index("col")
@@ -43,6 +43,14 @@
     is_server = ((row // 4) % 2 == chip % 2) & ((row // 2) % 2 == core)
     served_row = chip // 2 * 8 + row % 8
     quarter = row // 8
+    last = cols // 2 - 1
+
+    def first_of(place):
+        return place * (1 - place // last)
+
+    first_chip = first_of(home_chip)
+    at_first = chip == first_chip
+    is_first_self = at_first & (col == home_col)
     top = levels - 1
     half = fsend.shape[3]
     width = rhs.shape[-1]
@@ -121,14 +129,14 @@
 
         lax.fori_loop(0, count, body, 0)
 
-    @pl.when(at_home)
+    @pl.when(at_first)
     def _():
         for to_row in plane[:-1]:
             pl.semaphore_signal(barrier, inc=1, device_id=(to_row, home_col), device_id_type=MESH)
         greet((row, home_col))
 
     for h in range(2):
-        greet((row, home_chip * 2 + h))
+        greet((row, first_chip * 2 + h))
 
     def fold(later, earlier):
         index = pair_index(later, earlier)
@@ -156,12 +164,12 @@
         forward_out[level] = solved
         ebuf[level] = times(solved, diag[level])
 
-    def await_halves(buf, sem):
-        @pl.when(at_home)
+    def await_halves(buf, sem, has_one):
+        @pl.when(has_one)
         def _():
             await_recv(buf.at[0], sem)
 
-        @pl.when(jnp.logical_not(at_home))
+        @pl.when(jnp.logical_not(has_one))
         def _():
             await_recv(buf, sem)
 
@@ -193,21 +201,29 @@
             fsend[at, j] = lower[j].astype(BF16).reshape(2, half, width)
         if level == 1:
 
-            @pl.when(jnp.logical_not(at_home))
+            @pl.when(jnp.logical_not(at_first))
             def _():
                 pl.semaphore_wait(barrier, 4)
 
-            @pl.when(at_home & jnp.logical_not(is_self))
+            @pl.when(at_first & jnp.logical_not(is_first_self))
             def _():
                 pl.semaphore_wait(barrier, 4 + cols - 1)
 
-            @pl.when(is_self)
+            @pl.when(is_first_self)
             def _():
                 pl.semaphore_wait(barrier, 3 + cols - 1)
 
+        if level == 2:
+
+            @pl.when(chip == last)
+            def _():
+                pl.semaphore_wait(ready, 4)
+
+        to_chip = first_of(chip) if level == 1 else chip
         for j in range(2):
             for h in range(2):
-                send(fsend.at[at, j, h], arecv.at[at, row], a_send.at[at], a_recv.at[at], (2 * col + j, chip * 2 + h))
+                to = (2 * col + j, to_chip * 2 + h)
+                send(fsend.at[at, j, h], arecv.at[at, row], a_send.at[at], a_recv.at[at], to)
 
         if level == 1:
             loads[4].wait()
@@ -217,7 +233,7 @@
         early = [sum(fterm(level + 1, b, j) for b in range(level)) for j in range(2)]
         finish_forward(level - 1)
 
-        @pl.when(at_home)
+        @pl.when(at_first if level == 1 else at_home)
         def _():
             await_recv(arecv.at[at], a_recv.at[at])
             total = jnp.sum(arecv[at].astype(F32), axis=0)
@@ -226,8 +242,14 @@
             own = zbuf.at[level, core]
             for to_col in column[:-1]:
                 remote(own, own, b_send.at[at], b_recv.at[at], (row, to_col)).start()
-
-        await_halves(zbuf.at[level], b_recv.at[at])
+            if level == 1:
+
+                @pl.when(home_chip == last)
+                def _():
+                    for to_row in plane:
+                        pl.semaphore_signal(ready, inc=1, device_id=(to_row, home_col), device_id_type=MESH)
+
+        await_halves(zbuf.at[level], b_recv.at[at], at_first if level == 1 else at_home)
         lower = [early[j] + fterm(level + 1, level, j) for j in range(2)]
         if level == 1:
 
@@ -315,15 +337,13 @@
         pl.when(jnp.logical_not(one_less))(lambda: await_sends(count, sem, slots))
 
     for at in range(top - 1):
-        await_all_but(is_self, 4, a_send.at[at], arecv)
+        await_all_but(is_first_self if at == 0 else is_self, 4, a_send.at[at], arecv)
     await_all_but(is_server, 8, a_send.at[top - 1], rrecv)
     for level in range(1, top):
         await_all_but(is_self, 4, r_send.at[level], rrecv)
 
-    @pl.when(at_home)
-    def _():
-        for at in range(top - 1):
-            await_sends(cols - 1, b_send.at[at], arecv)
+    for at in range(top - 1):
+        pl.when(at_first if at == 0 else at_home)(lambda at=at: await_sends(cols - 1, b_send.at[at], arecv))
 
     @pl.when(is_server)
     def _():
@@ -389,7 +409,7 @@
         + [dma((steps,))] * 8
         + [dma((levels,))] * 2
         + [dma((6,))]
-        + [dma] * 2,
+        + [dma, dma, pltpu.SemaphoreType.REGULAR],
         compiler_params=pltpu.CompilerParams(collective_id=0, has_side_effects=True),
         name="solves",
     )(

time: 98.8 us -> 98.3 us (level)
  no operation moved by 1% of the time
where the time goes in v6:
time: 98.3 us; the launch traced here: 98.2 us
  Pallas kernels  97.5 us (99%)
    pallas_call x1, Pallas kernels, on_device(): pl.pallas_call(functools.partial(kernel, levels, rows, cols), out_shape=(...  96.9 us

profile of v6, /device:TPU:1, one launch (start us, length us, event | category | flops | bytes accessed | tf_op | source)
XLA Modules:
  0.0 98.2 jit_solution(6596373856621669463)
XLA Ops:
  0.6 96.9 %solves.1 = (bf16[5,32,256]{2,1,0:T(8,128)(2,1)S(1)}, bf16[5,32,256]{2,1,0:T(8,128)(2,1)S(1)}) custom-call(bf16[5,32,256]{2,1,0:T(8,128)(2,1)} %bitcast.12, bf16[20,256,256]{2,1,0:T(8,128)(2,1)} %bitcast.10, s32[2,1,10]{2,1,0:T(1,128)} %bitcast.13, bf16[5,256,256]{2,1,0:T(8,128)(2,1)} %bitcast.11), custom_call_target="tpu_custom_call" | custom-call | tf_op jit(solution)/shard_map/solves/pallas_call | solution.py:381
  97.5 0.7 results.1

commit v7 on v6

--- a/solution.py
+++ b/solution.py
@@ -16,12 +16,21 @@
     return later * (later - 1) // 2 + earlier
 
 
-def times_transposed(left, right):
-    return lax.dot_general(left, right, (((1,), (1,)), ((), ())), preferred_element_type=F32)
-
-
-def times(left, right):
-    return lax.dot_general(left, right, (((1,), (0,)), ((), ())), preferred_element_type=F32)
+def product(left, right, transposed, unit):
+    def run(total):
+        pltpu.matmul_push_rhs(right, 1, unit, transpose=transposed)
+        pltpu.matmul_acc_lhs(total, left, 1)
+        return pltpu.matmul_pop(total)
+
+    return pl.run_scoped(run, pltpu.ACC(unit)(left.shape, F32))
+
+
+def times_transposed(left, right, unit=0):
+    return product(left, right, True, unit)
+
+
+def times(left, right, unit=0):
+    return product(left, right, False, unit)
 
 
 def kernel(
@@ -141,11 +150,9 @@
     def fold(later, earlier):
         index = pair_index(later, earlier)
 
-        def one(j):
-            block = times(factor[2 * index + j], diag[earlier]) * pattern[j, 0, index].astype(F32)
+        for j in range(2):
+            block = times(factor[2 * index + j], diag[earlier], j) * pattern[j, 0, index].astype(F32)
             factor[2 * index + j] = block.astype(BF16)
-
-        repeat(2, one)
 
     def joined(ref):
         return ref[...].reshape(2 * half, width)
@@ -154,10 +161,23 @@
         return rhs[0] if level == 0 else joined(zbuf.at[level])
 
     def fterm(later, earlier, j):
-        return times_transposed(zeta_of(earlier), factor[2 * pair_index(later, earlier) + j])
+        return times_transposed(zeta_of(earlier), factor[2 * pair_index(later, earlier) + j], j)
 
     def bterm(later, earlier, j):
-        return times(joined(pbuf.at[later, j]), factor[2 * pair_index(later, earlier) + j])
+        return times(joined(pbuf.at[later, j]), factor[2 * pair_index(later, earlier) + j], j)
+
+    def prepare(later, earlier, transposed):
+        for j in range(2):
+            block = factor[2 * pair_index(later, earlier) + j]
+            pltpu.matmul_push_rhs(block, 0, j, transpose=transposed)
+
+    def prepared_times(lefts):
+        def run(*products):
+            for left, total in zip(lefts, products):
+                pltpu.matmul_acc_lhs(total, left, 0)
+            return [pltpu.matmul_pop(total) for total in products]
+
+        return pl.run_scoped(run, *[pltpu.ACC(j)((2 * half, width), F32) for j in range(2)])
 
     def finish_forward(level):
         solved = times_transposed(zeta_of(level), diag[level]).astype(BF16)
@@ -232,6 +252,7 @@
                 fold(later, earlier)
         early = [sum(fterm(level + 1, b, j) for b in range(level)) for j in range(2)]
         finish_forward(level - 1)
+        prepare(level + 1, level, True)
 
         @pl.when(at_first if level == 1 else at_home)
         def _():
@@ -250,7 +271,7 @@
                         pl.semaphore_signal(ready, inc=1, device_id=(to_row, home_col), device_id_type=MESH)
 
         await_halves(zbuf.at[level], b_recv.at[at], at_first if level == 1 else at_home)
-        lower = [early[j] + fterm(level + 1, level, j) for j in range(2)]
+        lower = [early[j] + term for j, term in enumerate(prepared_times([zeta_of(level)] * 2))]
         if level == 1:
 
             @pl.when(is_self)
@@ -273,15 +294,17 @@
         await_recv(dtop, d_recv)
         await_recv(atop, a_recv.at[at])
         zeta = jnp.sum(atop[...].astype(F32), axis=0).astype(BF16)
-        fq[...] = times_transposed(zeta, dtop[...]).astype(BF16)
-        sq[top] = times(fq[...], dtop[...]).astype(BF16)
+        twice = times_transposed(jnp.concatenate([zeta, zeta], axis=0), dtop[...]).astype(BF16)
+        fq[...] = twice[: half // 2]
+        sq[top] = times(twice, dtop[...])[: half // 2].astype(BF16)
         serve(top)
         give(fq, ftop.at[quarter], b_send.at[at], b_recv.at[at])
 
     early = None
     for level in range(top - 1, -1, -1):
+        prepare(level + 1, level, False)
         await_recv(pbuf.at[level + 1], p_recv.at[level])
-        upper = bterm(level + 1, level, 0) + bterm(level + 1, level, 1)
+        upper = sum(prepared_times([joined(pbuf.at[level + 1, j]) for j in range(2)]))
         if early is not None:
             upper = upper + early
         if level > 0:

time: 98.3 us -> 97.8 us (level)
  no operation moved by 1% of the time
where the time goes in v7:
time: 97.8 us; the launch traced here: 97.6 us
  Pallas kernels  97 us (99%)
    pallas_call x1, Pallas kernels, on_device(): pl.pallas_call(functools.partial(kernel, levels, rows, cols), out_shape=(...  96.3 us

profile of v7, /device:TPU:1, one launch (start us, length us, event | category | flops | bytes accessed | tf_op | source)
XLA Modules:
  0.0 97.6 jit_solution(18181541045031024246)
XLA Ops:
  0.6 96.3 %solves.1 = (bf16[5,32,256]{2,1,0:T(8,128)(2,1)S(1)}, bf16[5,32,256]{2,1,0:T(8,128)(2,1)S(1)}) custom-call(bf16[5,32,256]{2,1,0:T(8,128)(2,1)} %bitcast.12, bf16[20,256,256]{2,1,0:T(8,128)(2,1)} %bitcast.10, s32[2,1,10]{2,1,0:T(1,128)} %bitcast.13, bf16[5,256,256]{2,1,0:T(8,128)(2,1)} %bitcast.11), custom_call_target="tpu_custom_call" | custom-call | tf_op jit(solution)/shard_map/solves/pallas_call | solution.py:404
  97.0 0.7 results.1
